TPU v7x, 32 devices: a whole 2x2x4 slice. The times are simulated.
32 devices in a mesh: seq: 16 (over z, x, core), mlp: 2 (over y).
Axes of the slice: x: 2, y: 2, z: 4, core: 2. Of those that a mesh axis runs over, the one named last changes fastest.
Arguments:
- patches: bfloat16 [16384, 768], P(('seq', 'mlp')), may hold values from -6 to 6
- segments: int32 [16384], P(('seq', 'mlp')), may hold values from 0 to 5, as said below
- prompt_slots: int32 [16384], P(('seq', 'mlp')), may hold values from 0 to 50, as said below
- norm_gains: float32 [2, 2, 768], replicated, may hold values from 0.25 to 1.75
- qkv_weight: bfloat16 [2, 768, 2304], P(None, 'seq'), may hold values from -0.21875 to 0.21875
- out_weight: bfloat16 [2, 768, 768], P(None, 'seq'), may hold values from -0.875 to 0.875
- up_weight: bfloat16 [2, 768, 3072], P(None, 'seq', 'mlp'), may hold values from -0.21875 to 0.21875
- down_weight: bfloat16 [2, 3072, 768], P(None, 'mlp', 'seq'), may hold values from -0.15625 to 0.15625
- cotangent: bfloat16 [16384, 768], P(('seq', 'mlp')), may hold values from -6 to 6
- prompts: float32 [76800], P(('seq', 'mlp')), may hold values from -5 to 5
- first_moment: float32 [76800], P(('seq', 'mlp')), may hold values from -0.24 to 0.24
- second_moment: float32 [76800], P(('seq', 'mlp')), may hold values from 1e-05 to 0.015
- adam_betas: float32 [2], replicated, may hold values from 0.4 to 0.6
- learn_rate: float32 [1], replicated, may hold values from 0.2 to 0.6
Outputs:
- block_output: bfloat16 [16384, 768], P(('seq', 'mlp'))
- input_grad: float32 [16384, 768], P(('seq', 'mlp'))
- new_prompts: float32 [76800], P(('seq', 'mlp'))
- new_first: float32 [76800], P(('seq', 'mlp'))
- new_second: float32 [76800], P(('seq', 'mlp'))
- grad_norm: float32 [1], replicated
Inputs may be any that keep to these rules, and one draw needn't show every extreme that they name: `segments`: the 512 tokens of one device form aligned blocks in which whole images lie one after another, numbered 0, 1, 2 and so on; each image has 51 to 247 tokens, and every block holds an image of exactly 247 tokens. `prompt_slots`: the first 50 tokens of each image hold slots 0 to 49 in order; all other tokens hold 50.
All inputs are finite; a program needn't handle non-finite values.
Results may differ from a plain program's by a relative error of at most 0.02.
Values may be sent and summed in bfloat16 or wider, within the bound.
No kernel may reach another device: no remote copies, remote signals or barrier semaphores. Data moves between devices by JAX's collectives and lax.ppermute only.
A program may use at most 192 MiB of HBM per device.

v0:
```python
from functools import partial
import math

import jax
import jax.numpy as jnp
from jax import lax
from jax.sharding import PartitionSpec as P

HEADS = 12
HEAD_DIM = 64
ADAM_STEP = 2


ln_eps = 1e-06
masked_score = -1e30
clip_ratio = 0.05
adam_eps = 1e-08
decay_rate = 0.1
highest = lax.Precision.HIGHEST


def layer_norm(values, gain_row):
    center = values - jnp.mean(values, axis=-1, keepdims=True)
    spread = jnp.mean(center * center, axis=-1, keepdims=True)
    return center * lax.rsqrt(spread + ln_eps) * gain_row


def exact_gelu(values):
    return jax.nn.gelu(values, approximate=False)


def rows_times(piece_rows, weight):
    return jnp.dot(piece_rows, weight, preferred_element_type=jnp.float32)


def rows_times_back(piece_rows, weight):
    return jnp.einsum("td,fd->tf", piece_rows, weight, preferred_element_type=jnp.float32)


def slice_times(source, weight):
    return jnp.dot(source, weight, preferred_element_type=jnp.float32)


def slice_times_back(source, weight):
    return jnp.einsum("tf,df->td", source, weight, preferred_element_type=jnp.float32)


def masked_scores(query_rows, key_heads, seg_query, segments, score_scale):
    raw_scores = (
        jnp.einsum("qhd,khd->hqk", query_rows, key_heads, preferred_element_type=jnp.float32)
        * score_scale
    )
    allowed = (seg_query[:, None] == segments[None, :])[None]
    return jnp.where(allowed, raw_scores, masked_score)


def attend_forward(query_heads, key_heads, value_heads, segments, score_scale):
    tokens, head_count, head_depth = query_heads.shape
    block_rows = min(512, tokens)
    blocks = tokens // block_rows
    query_blocks = query_heads.reshape(blocks, block_rows, head_count, head_depth)
    seg_blocks = segments.reshape(blocks, block_rows)

    def one_block(block_pair):
        query_rows, seg_query = block_pair
        scores = masked_scores(query_rows, key_heads, seg_query, segments, score_scale)
        row_max = jnp.max(scores, axis=2, keepdims=True)
        exponent = jnp.exp(scores - row_max)
        row_total = jnp.sum(exponent, axis=2, keepdims=True)
        attn_probs = (exponent / row_total).astype(jnp.bfloat16)
        mixed_heads = jnp.einsum(
            "hqk,khd->qhd", attn_probs, value_heads, preferred_element_type=jnp.float32
        )
        return (mixed_heads.astype(jnp.bfloat16), row_max + jnp.log(row_total))

    mixed_heads, block_lse = lax.map(one_block, (query_blocks, seg_blocks))
    return (mixed_heads.reshape(tokens, head_count * head_depth), block_lse)


def attend_backward(
    query_heads, key_heads, value_heads, segments, block_lse, grad_mixed, score_scale
):
    tokens, head_count, head_depth = query_heads.shape
    block_rows = min(512, tokens)
    blocks = tokens // block_rows
    query_blocks = query_heads.reshape(blocks, block_rows, head_count, head_depth)
    grad_blocks = grad_mixed.reshape(blocks, block_rows, head_count, head_depth)
    seg_blocks = segments.reshape(blocks, block_rows)

    def one_block(running, block_parts):
        grad_keys, grad_values = running
        query_rows, grad_rows, seg_query, row_lse = block_parts
        scores = masked_scores(query_rows, key_heads, seg_query, segments, score_scale)
        attn_probs = jnp.exp(scores - row_lse)
        grad_probs = jnp.einsum(
            "qhd,khd->hqk", grad_rows, value_heads, preferred_element_type=jnp.float32
        )
        inner_sum = jnp.sum(attn_probs * grad_probs, axis=2, keepdims=True)
        grad_scores = (attn_probs * (grad_probs - inner_sum)).astype(jnp.bfloat16)
        grad_query = (
            jnp.einsum("hqk,khd->qhd", grad_scores, key_heads, preferred_element_type=jnp.float32)
            * score_scale
        )
        grad_keys = (
            grad_keys
            + jnp.einsum(
                "hqk,qhd->khd", grad_scores, query_rows, preferred_element_type=jnp.float32
            )
            * score_scale
        )
        grad_values = grad_values + jnp.einsum(
            "hqk,qhd->khd",
            attn_probs.astype(jnp.bfloat16),
            grad_rows,
            preferred_element_type=jnp.float32,
        )
        return ((grad_keys, grad_values), grad_query)

    zero_grads = jnp.zeros((tokens, head_count, head_depth), jnp.float32)
    (grad_keys, grad_values), grad_query = lax.scan(
        one_block, (zero_grads, zero_grads), (query_blocks, grad_blocks, seg_blocks, block_lse)
    )
    return (
        grad_query.reshape(tokens, head_count * head_depth),
        grad_keys.reshape(tokens, -1),
        grad_values.reshape(tokens, -1),
    )


def per_device(
    patches,
    segments,
    prompt_slots,
    norm_gains,
    qkv_weight,
    out_weight,
    up_weight,
    down_weight,
    cotangent,
    prompts,
    first_moment,
    second_moment,
    adam_betas,
    learn_rate,
):
    layers = norm_gains.shape[0]
    feature_width = norm_gains.shape[2]
    tokens = patches.shape[0]
    score_scale = HEAD_DIM ** (-0.5)
    gathered = lax.all_gather(prompts, ("seq", "mlp"), axis=0, tiled=True)
    prompt_table = gathered.reshape(layers, -1, feature_width)
    slot_total = prompt_table.shape[1]
    w_qkv, w_out, w_up, w_down = (
        lax.all_gather(qkv_weight, "seq", axis=1, tiled=True),
        lax.all_gather(out_weight, "seq", axis=1, tiled=True),
        lax.all_gather(up_weight, "seq", axis=1, tiled=True),
        lax.all_gather(down_weight, "seq", axis=2, tiled=True),
    )
    onehot = (prompt_slots[:, None] == jnp.arange(slot_total)[None, :]).astype(jnp.float32)
    is_prompt = (prompt_slots < slot_total)[:, None]
    hidden = patches.astype(jnp.float32)
    kept_state = []
    for layer_at in range(layers):
        inject = jnp.dot(onehot, prompt_table[layer_at], precision=highest)
        entry_rows = jnp.where(is_prompt, inject, hidden)
        normed_one, norm_one_back = jax.vjp(
            partial(layer_norm, gain_row=norm_gains[layer_at, 0]), entry_rows
        )
        qkv_proj = jnp.dot(
            normed_one.astype(jnp.bfloat16), w_qkv[layer_at], preferred_element_type=jnp.float32
        ).astype(jnp.bfloat16)
        query_heads = qkv_proj[:, :feature_width].reshape(tokens, HEADS, HEAD_DIM)
        key_heads = qkv_proj[:, feature_width : 2 * feature_width].reshape(tokens, HEADS, HEAD_DIM)
        value_heads = qkv_proj[:, 2 * feature_width :].reshape(tokens, HEADS, HEAD_DIM)
        mixed_rows, block_lse = attend_forward(
            query_heads, key_heads, value_heads, segments, score_scale
        )
        middle = entry_rows + jnp.dot(
            mixed_rows, w_out[layer_at], preferred_element_type=jnp.float32
        )
        normed_two, norm_two_back = jax.vjp(
            partial(layer_norm, gain_row=norm_gains[layer_at, 1]), middle
        )
        normed_low = normed_two.astype(jnp.bfloat16)
        before = rows_times(
            lax.all_gather(normed_low, "mlp", axis=0, tiled=True), weight=w_up[layer_at]
        )
        active = exact_gelu(before).astype(jnp.bfloat16)
        branch_two = lax.psum_scatter(
            slice_times(source=active, weight=w_down[layer_at]).astype(jnp.bfloat16),
            "mlp",
            scatter_dimension=0,
            tiled=True,
        ).astype(jnp.float32)
        hidden = middle + branch_two
        kept_state.append(
            (query_heads, key_heads, value_heads, block_lse, norm_one_back, norm_two_back, before)
        )
    block_output = hidden.astype(jnp.bfloat16)
    gradient = cotangent.astype(jnp.float32)
    layer_grads = []
    for layer_at in reversed(range(layers)):
        query_heads, key_heads, value_heads, block_lse, norm_one_back, norm_two_back, before = (
            kept_state[layer_at]
        )
        grad_low = gradient.astype(jnp.bfloat16)
        grad_active = rows_times_back(
            lax.all_gather(grad_low, "mlp", axis=0, tiled=True), weight=w_down[layer_at]
        )
        gelu_back = jax.vjp(exact_gelu, before)[1]
        grad_before = gelu_back(grad_active)[0].astype(jnp.bfloat16)
        grad_normtwo = lax.psum_scatter(
            slice_times_back(source=grad_before, weight=w_up[layer_at]).astype(jnp.bfloat16),
            "mlp",
            scatter_dimension=0,
            tiled=True,
        ).astype(jnp.float32)
        grad_middle = gradient + norm_two_back(grad_normtwo)[0]
        grad_branch = grad_middle.astype(jnp.bfloat16)
        grad_mixed = jnp.einsum(
            "te,de->td", grad_branch, w_out[layer_at], preferred_element_type=jnp.float32
        ).astype(jnp.bfloat16)
        grad_query, grad_keys, grad_values = attend_backward(
            query_heads,
            key_heads,
            value_heads,
            segments,
            block_lse,
            grad_mixed.reshape(tokens, HEADS, HEAD_DIM),
            score_scale,
        )
        grad_qkv = jnp.concatenate([grad_query, grad_keys, grad_values], axis=1).astype(
            jnp.bfloat16
        )
        grad_normone = jnp.einsum(
            "tc,dc->td", grad_qkv, w_qkv[layer_at], preferred_element_type=jnp.float32
        )
        grad_entry = grad_middle + norm_one_back(grad_normone)[0]
        layer_grads.append(jnp.einsum("tp,td->pd", onehot, grad_entry, precision=highest))
        gradient = jnp.where(is_prompt, 0.0, grad_entry)
    local_grads = jnp.stack(layer_grads[::-1]).reshape(-1)
    own_grads = lax.psum_scatter(local_grads, ("seq", "mlp"), scatter_dimension=0, tiled=True)
    square_sum = lax.psum(jnp.sum(own_grads * own_grads), ("seq", "mlp"))
    grad_norm = jnp.sqrt(square_sum)
    clip_limit = clip_ratio * math.sqrt(local_grads.shape[0])
    clipped = own_grads * jnp.minimum(1.0, clip_limit / (grad_norm + 1e-06))
    beta_one = adam_betas[0]
    beta_two = adam_betas[1]
    step_value = float(ADAM_STEP)
    new_first = beta_one * first_moment + (1.0 - beta_one) * clipped
    new_second = beta_two * second_moment + (1.0 - beta_two) * clipped * clipped
    first_hat = new_first / (1.0 - beta_one**step_value)
    second_hat = new_second / (1.0 - beta_two**step_value)
    new_prompts = prompts - learn_rate[0] * (
        first_hat / (jnp.sqrt(second_hat) + adam_eps) + decay_rate * prompts
    )
    return (block_output, gradient, new_prompts, new_first, new_second, grad_norm.reshape(1))


def solution(mesh):
    in_specs = (
        P(("seq", "mlp"), None),
        P(("seq", "mlp")),
        P(("seq", "mlp")),
        P(),
        P(None, "seq", None),
        P(None, "seq", None),
        P(None, "seq", "mlp"),
        P(None, "mlp", "seq"),
        P(("seq", "mlp"), None),
        P(("seq", "mlp")),
        P(("seq", "mlp")),
        P(("seq", "mlp")),
        P(),
        P(),
    )
    out_specs = (
        P(("seq", "mlp"), None),
        P(("seq", "mlp"), None),
        P(("seq", "mlp")),
        P(("seq", "mlp")),
        P(("seq", "mlp")),
        P(),
    )
    return jax.shard_map(
        per_device, mesh=mesh, in_specs=in_specs, out_specs=out_specs, check_vma=False
    )
```

profile of v0, /device:TPU:1, one launch (start us, length us, event | category | flops | bytes accessed | tf_op | source)
XLA Modules:
  0.0 814.3 jit_solution(11228677048224738187)
XLA Ops:
  14.0 173.2 %all-reduce.5.cloned.1.call-done = f32[76800]{0:T(1024)} async-done(((f32[76800]{0:T(1024)}), f32[76800]{0:T(1024)}) %all-reduce.5.cloned.1.call-update) | async-done | bytes 307216
  191.4 4.3 convolution_convert_fusion.1
  199.0 2.6 copy.60
  208.2 4.5 fusion.59
  217.8 27.8 %all-gather.13.cloned.1.call-done = bf16[1024,768]{1,0:T(8,128)(2,1)} async-done(((bf16[512,768]{1,0:T(8,128)(2,1)}), bf16[1024,768]{1,0:T(8,128)(2,1)}) %all-gather.13.cloned.1.call-update) | async-done | bytes 1572880 | tf_op jit(solution)/shard_map/all_gather | solution.py:186
  245.6 19.2 %fusion.4 = (f32[1024,1536]{1,0:T(8,128)}, f32[1024,1536]{1,0:T(8,128)}) fusion(bf16[1024,768]{1,0:T(8,128)(2,1)} %all-gather.13.cloned.1.call-done, bf16[2,768,1536]{2,1,0:T(8,128)(2,1)} %all-gather.15.cloned.1.call-done), kind=kOutput, calls=%fused_computation.18 | convolution fusion | flops 2513436672 | bytes 16515072 | tf_op jit(solution)/shard_map/dot_general | solution.py:33
  264.8 37.0 %all-gather.17.cloned.1.call-done = bf16[2,1536,768]{1,2,0:T(8,128)(2,1)} async-done(((bf16[2,1536,48]{1,2,0:T(8,128)(2,1)}), bf16[2,1536,768]{1,2,0:T(8,128)(2,1)}) %all-gather.17.cloned.1.call-update) | async-done | bytes 4718608 | tf_op jit(solution)/shard_map/all_gather | solution.py:157
  301.8 9.1 %fusion.51 = bf16[1024,768]{1,0:T(8,128)(2,1)} fusion(bf16[2,1536,768]{1,2,0:T(8,128)(2,1)} %all-gather.17.cloned.1.call-done, f32[1024,1536]{1,0:T(8,128)} %get-tuple-element.152, f32[1024,1536]{1,0:T(8,128)} %get-tuple-element.153), kind=kOutput, calls=%fused_computation.95 | convolution fusion | flops 2421424128 | bytes 16515072 | tf_op jit(solution)/shard_map/dot_general | solution.py:41
  311.2 23.8 %reduce-scatter.5.cloned.1.call-done = bf16[512,768]{1,0:T(8,128)(2,1)} async-done(((bf16[1024,768]{1,0:T(8,128)(2,1)}), bf16[512,768]{1,0:T(8,128)(2,1)}) %reduce-scatter.5.cloned.1.call-update) | async-done | bytes 786448 | tf_op jit(solution)/shard_map/reduce_scatter | solution.py:189
  337.5 4.3 convolution_convert_fusion
  354.4 3.6 fusion.58
  361.4 26.1 %all-gather.19.cloned.1.call-done = bf16[1024,768]{1,0:T(8,128)(2,1)} async-done(((bf16[512,768]{1,0:T(8,128)(2,1)}), bf16[1024,768]{1,0:T(8,128)(2,1)}) %all-gather.19.cloned.1.call-update) | async-done | bytes 1572880 | tf_op jit(solution)/shard_map/all_gather | solution.py:186
  387.6 18.9 %fusion.5 = (f32[1024,1536]{1,0:T(8,128)}, f32[1024,1536]{1,0:T(8,128)}) fusion(bf16[1024,768]{1,0:T(8,128)(2,1)} %all-gather.19.cloned.1.call-done, bf16[2,768,1536]{2,1,0:T(8,128)(2,1)} %all-gather.15.cloned.1.call-done), kind=kOutput, calls=%fused_computation.19 | convolution fusion | flops 2513436672 | bytes 16515072 | tf_op jit(solution)/shard_map/dot_general | solution.py:33
  406.4 9.7 %all-gather.21.cloned.1.call-done = bf16[1024,768]{1,0:T(8,128)(2,1)} async-done(((bf16[512,768]{1,0:T(8,128)(2,1)}), bf16[1024,768]{1,0:T(8,128)(2,1)}) %all-gather.21.cloned.1.call-update) | async-done | bytes 1572880 | tf_op jit(solution)/shard_map/all_gather | solution.py:208
  416.1 13.0 %fusion.49 = bf16[1024,768]{1,0:T(8,128)(2,1)} fusion(bf16[2,768,1536]{2,1,0:T(8,128)(2,1)} %all-gather.15.cloned.1.call-done, f32[1024,1536]{1,0:T(8,128)} %get-tuple-element.160, f32[1024,1536]{1,0:T(8,128)} %get-tuple-element.161, bf16[1024,768]{1,0:T(8,128)(2,1)} %all-gather.21.cloned.1.call-done, bf16[2,1536,768]{1,2,0:T(8,128)(2,1)} %all-gather.17.cloned.1.call-done), kind=kOutput, calls=%fused_computation.93 | convolution fusion | flops 4854644736 | bytes 20447232 | tf_op jit(solution)/shard_map/tf,df->td/dot_general | solution.py:45
  429.1 9.1 %fusion.50 = bf16[1024,768]{1,0:T(8,128)(2,1)} fusion(bf16[2,1536,768]{1,2,0:T(8,128)(2,1)} %all-gather.17.cloned.1.call-done, f32[1024,1536]{1,0:T(8,128)} %get-tuple-element.160, f32[1024,1536]{1,0:T(8,128)} %get-tuple-element.161), kind=kOutput, calls=%fused_computation.94 | convolution fusion | flops 2421424128 | bytes 16515072 | tf_op jit(solution)/shard_map/dot_general | solution.py:41
  438.5 16.7 %reduce-scatter.9.cloned.1.call-done = bf16[512,768]{1,0:T(8,128)(2,1)} async-done(((bf16[1024,768]{1,0:T(8,128)(2,1)}), bf16[512,768]{1,0:T(8,128)(2,1)}) %reduce-scatter.9.cloned.1.call-update) | async-done | bytes 786448 | tf_op jit(solution)/shard_map/reduce_scatter | solution.py:212
  456.7 26.8 %reduce-scatter.7.cloned.1.call-done = bf16[512,768]{1,0:T(8,128)(2,1)} async-done(((bf16[1024,768]{1,0:T(8,128)(2,1)}), bf16[512,768]{1,0:T(8,128)(2,1)}) %reduce-scatter.7.cloned.1.call-update) | async-done | bytes 786448 | tf_op jit(solution)/shard_map/reduce_scatter | solution.py:189
  483.5 2.9 fusion.101
  490.3 7.3 fusion.52
  497.7 9.6 %multiply_reduce_fusion.1 = (f32[12,512]{1,0:T(8,128)S(1)}, f32[12,512,512]{1,2,0:T(8,128)}) fusion(f32[12,512]{1,0:T(8,128)S(1)} %log_add_fusion.1, f32[12,512,512]{1,2,0:T(8,128)} %copy-done.1, pred[512,512]{0,1:T(8,128)(4,1)S(1)} %broadcast_compare_fusion, bf16[512,12,64]{0,2,1:T(8,128)(2,1)S(1)} %bitcast.151, bf16[512,12,64]{0,2,1:T(8,128)(2,1)S(1)} %bitcast.149), kind=kOutput, calls=%fused_computation.4 | convolution fusion | flops 418375680 | bytes 27049984 | tf_op jit(solution)/shard_map/while/body/eval_jaxpr/qhd,khd->hqk/dot_general | solution.py:95
  507.3 7.1 multiply_convert_fusion.1
  523.6 26.8 %all-gather.23.cloned.1.call-done = bf16[1024,768]{1,0:T(8,128)(2,1)} async-done(((bf16[512,768]{1,0:T(8,128)(2,1)}), bf16[1024,768]{1,0:T(8,128)(2,1)}) %all-gather.23.cloned.1.call-update) | async-done | bytes 1572880 | tf_op jit(solution)/shard_map/all_gather | solution.py:208
  550.4 13.0 %fusion.48 = bf16[1024,768]{1,0:T(8,128)(2,1)} fusion(bf16[2,768,1536]{2,1,0:T(8,128)(2,1)} %all-gather.15.cloned.1.call-done, f32[1024,1536]{1,0:T(8,128)} %get-tuple-element.152, f32[1024,1536]{1,0:T(8,128)} %get-tuple-element.153, bf16[1024,768]{1,0:T(8,128)(2,1)} %all-gather.23.cloned.1.call-done, bf16[2,1536,768]{1,2,0:T(8,128)(2,1)} %all-gather.17.cloned.1.call-done), kind=kOutput, calls=%fused_computation.92 | convolution fusion | flops 4854644736 | bytes 20447232 | tf_op jit(solution)/shard_map/tf,df->td/dot_general | solution.py:45
  565.0 24.5 %reduce-scatter.11.cloned.1.call-done = bf16[512,768]{1,0:T(8,128)(2,1)} async-done(((bf16[1024,768]{1,0:T(8,128)(2,1)}), bf16[512,768]{1,0:T(8,128)(2,1)}) %reduce-scatter.11.cloned.1.call-update) | async-done | bytes 786448 | tf_op jit(solution)/shard_map/reduce_scatter | solution.py:212
  596.4 7.6 fusion.55
  604.0 9.5 %multiply_reduce_fusion = (f32[12,512]{1,0:T(8,128)S(1)}, f32[12,512,512]{1,2,0:T(8,128)}) fusion(f32[12,512]{1,0:T(8,128)S(1)} %log_add_fusion, f32[12,512,512]{1,2,0:T(8,128)} %copy-done, pred[512,512]{0,1:T(8,128)(4,1)S(1)} %broadcast_compare_fusion, bf16[512,12,64]{0,2,1:T(8,128)(2,1)S(1)} %bitcast.153, bf16[512,12,64]{0,2,1:T(8,128)(2,1)S(1)} %bitcast.147), kind=kOutput, calls=%fused_computation.1 | convolution fusion | flops 418375680 | bytes 27049984 | tf_op jit(solution)/shard_map/while/body/eval_jaxpr/qhd,khd->hqk/dot_general | solution.py:95
  613.5 7.1 multiply_convert_fusion
  636.1 120.3 %all-reduce.7.cloned.1.call-done = f32[76800]{0:T(1024)} async-done(((f32[76800]{0:T(1024)}), f32[76800]{0:T(1024)}) %all-reduce.7.cloned.1.call-update) | async-done | bytes 307216
  757.8 2.8 broadcast_select_fusion
  760.6 41.3 %psum.7 = f32[]{:T(128)} all-reduce(f32[]{:T(128)} %multiply_reduce_fusion.10), channel_id=1, replica_groups=mesh['seq'=16,'mlp'=2] {'seq','mlp'}, use_global_device_ids=true, to_apply=%region_28.29 | all-reduce | flops 1 | bytes 8 | tf_op jit(solution)/shard_map/psum | solution.py:243
  802.7 2.7 multiply_subtract_fusion
  (237 shorter events, 78.8 us)
Async XLA Ops:
  8.0 179.2 %all-reduce.5.cloned.1.call-start = ((), (), s32[]{:S(2)}) async-start(), calls=%async_computation.16 | async-start | bytes 614400
  9.7 181.7 %all-gather.9.cloned.1.call-start = ((), (), s32[]{:S(2)}) async-start(), calls=%async_computation.4 | async-start | bytes 7520256 | tf_op jit(solution)/shard_map/all_gather | solution.py:154
  10.3 202.4 %all-gather.11.cloned.1.call-start = ((), (), s32[]{:S(2)}) async-start(), calls=%async_computation.5 | async-start | bytes 2506752 | tf_op jit(solution)/shard_map/all_gather | solution.py:155
  10.9 206.8 %all-gather.15.cloned.1.call-start = ((), (), s32[]{:S(2)}) async-start(), calls=%async_computation.7 | async-start | bytes 5013504 | tf_op jit(solution)/shard_map/all_gather | solution.py:156
  11.5 234.1 %all-gather.13.cloned.1.call-start = ((), (), s32[]{:S(2)}) async-start(), calls=%async_computation.6 | async-start | bytes 2359296 | tf_op jit(solution)/shard_map/all_gather | solution.py:186
  12.4 183.3 %copy-start.47 = (f32[768]{0:T(1024)}, f32[768]{0:T(1024)S(1)}, u32[]{:S(2)}) copy-start(f32[768]{0:T(1024)S(1)} %get-tuple-element.89) | copy-start | bytes 9220
  12.4 203.2 %copy-start.33 = (f32[768]{0:T(1024)}, f32[768]{0:T(1024)S(1)}, u32[]{:S(2)}) copy-start(f32[768]{0:T(1024)S(1)} %get-tuple-element.88) | copy-start | bytes 9220
  191.0 21.7 %copy-start.5 = (f32[512,768]{1,0:T(8,128)}, f32[512,768]{1,0:T(8,128)S(1)}, u32[]{:S(2)}) copy-start(f32[512,768]{1,0:T(8,128)S(1)} %get-tuple-element.136) | copy-start | bytes 4718596
  215.5 49.3 %copy-start.45 = (f32[512]{0:T(512)}, f32[512]{0:T(512)S(1)}, u32[]{:S(2)}) copy-start(f32[512]{0:T(512)S(1)} %multiply_reduce_fusion.8) | copy-start | bytes 6148
  215.5 49.3 %copy-start.39 = (f32[512]{0:T(512)}, f32[512]{0:T(512)S(1)}, u32[]{:S(2)}) copy-start(f32[512]{0:T(512)S(1)} %fusion.76) | copy-start | bytes 6148
  216.9 84.8 %all-gather.17.cloned.1.call-start = ((), (), s32[]{:S(2)}) async-start(), calls=%async_computation.8 | async-start | bytes 5013504 | tf_op jit(solution)/shard_map/all_gather | solution.py:157
  217.7 117.3 %reduce-scatter.5.cloned.1.call-start = ((), (), s32[]{:S(2)}) async-start(), calls=%async_computation.9 | async-start | bytes 2359296 | tf_op jit(solution)/shard_map/reduce_scatter | solution.py:189
  301.8 33.2 %copy-start.37 = (s32[512]{0:T(512)S(1)}, s32[512]{0:T(512)}, u32[]{:S(2)}) copy-start(s32[512]{0:T(512)} %param.16) | copy-start | bytes 6148
  310.9 76.6 %all-gather.19.cloned.1.call-start = ((), (), s32[]{:S(2)}) async-start(), calls=%async_computation.10 | async-start | bytes 2359296 | tf_op jit(solution)/shard_map/all_gather | solution.py:186
  360.4 55.7 %all-gather.21.cloned.1.call-start = ((), (), s32[]{:S(2)}) async-start(), calls=%async_computation.12 | async-start | bytes 2359296 | tf_op jit(solution)/shard_map/all_gather | solution.py:208
  361.0 94.2 %reduce-scatter.9.cloned.1.call-start = ((), (), s32[]{:S(2)}) async-start(), calls=%async_computation.13 | async-start | bytes 2359296 | tf_op jit(solution)/shard_map/reduce_scatter | solution.py:212
  429.1 54.4 %reduce-scatter.7.cloned.1.call-start = ((), (), s32[]{:S(2)}) async-start(), calls=%async_computation.11 | async-start | bytes 2359296 | tf_op jit(solution)/shard_map/reduce_scatter | solution.py:189
  438.2 112.2 %all-gather.23.cloned.1.call-start = ((), (), s32[]{:S(2)}) async-start(), calls=%async_computation.14 | async-start | bytes 2359296 | tf_op jit(solution)/shard_map/all_gather | solution.py:208
  523.3 40.3 %copy-start.8 = (f32[512,768]{1,0:T(8,128)}, f32[512,768]{1,0:T(8,128)S(1)}, u32[]{:S(2)}) copy-start(f32[512,768]{1,0:T(8,128)S(1)} %get-tuple-element.108) | copy-start | bytes 4718596
  523.3 40.2 %copy-start.30 = (f32[12,512]{1,0:T(8,128)S(1)}, f32[12,512]{1,0:T(8,128)}, u32[]{:S(2)}) copy-start(f32[12,512]{1,0:T(8,128)} %copy-done.29) | copy-start | bytes 73732
  523.3 40.2 %copy-start.32 = (f32[12,512]{1,0:T(8,128)S(1)}, f32[12,512]{1,0:T(8,128)}, u32[]{:S(2)}) copy-start(f32[12,512]{1,0:T(8,128)} %copy-done.31) | copy-start | bytes 73732
  523.3 66.2 %copy-start.34 = (f32[768]{0:T(1024)S(1)}, f32[768]{0:T(1024)}, u32[]{:S(2)}) copy-start(f32[768]{0:T(1024)} %copy-done.33) | copy-start | bytes 9220
  523.3 66.2 %copy-start.36 = (f32[512]{0:T(512)S(1)}, f32[512]{0:T(512)}, u32[]{:S(2)}) copy-start(f32[512]{0:T(512)} %copy-done.35) | copy-start | bytes 6148
  523.3 67.9 %copy-start.46 = (f32[512]{0:T(512)S(1)}, f32[512]{0:T(512)}, u32[]{:S(2)}) copy-start(f32[512]{0:T(512)} %copy-done.45) | copy-start | bytes 6148
  523.3 67.9 %copy-start.40 = (f32[512]{0:T(512)S(1)}, f32[512]{0:T(512)}, u32[]{:S(2)}) copy-start(f32[512]{0:T(512)} %copy-done.39) | copy-start | bytes 6148
  523.3 66.2 %reduce-scatter.11.cloned.1.call-start = ((), (), s32[]{:S(2)}) async-start(), calls=%async_computation.15 | async-start | bytes 2359296 | tf_op jit(solution)/shard_map/reduce_scatter | solution.py:212
  563.4 192.9 %all-reduce.7.cloned.1.call-start = ((), (), s32[]{:S(2)}) async-start(), calls=%async_computation.17 | async-start | bytes 614400
  596.4 17.1 %slice-start = ((s8[12582912]{0:T(1024)(128)(4,1)}), s8[4194304]{0:T(1024)(128)(4,1)S(1)}, s32[]{:S(2)}) async-start(s8[12582912]{0:T(1024)(128)(4,1)} %bitcast.134), calls=%async_computation.18 | async-start | bytes 8388608
  596.4 17.1 %slice-start.1 = ((s8[12582912]{0:T(1024)(128)(4,1)}), s8[4194304]{0:T(1024)(128)(4,1)S(1)}, s32[]{:S(2)}) async-start(s8[12582912]{0:T(1024)(128)(4,1)} %bitcast.134), calls=%async_computation.19 | async-start | bytes 8388608
  627.5 175.2 %copy-start.38 = (f32[2400]{0:T(1024)S(1)}, f32[2400]{0:T(1024)}, u32[]{:S(2)}) copy-start(f32[2400]{0:T(1024)} %param.23) | copy-start | bytes 28804
  627.5 175.2 %copy-start.49 = (f32[2400]{0:T(1024)S(1)}, f32[2400]{0:T(1024)}, u32[]{:S(2)}) copy-start(f32[2400]{0:T(1024)} %param.25) | copy-start | bytes 28804
  627.5 175.2 %copy-start.50 = (f32[2400]{0:T(1024)S(1)}, f32[2400]{0:T(1024)}, u32[]{:S(2)}) copy-start(f32[2400]{0:T(1024)} %param.24) | copy-start | bytes 28804
  (48 other events, 218.4 us)
Sparse Core Ops, SparseCore 0:
  14.8 172.4 all-reduce.4
  631.2 125.1 all-reduce.6
Sparse Core Ops, SparseCore 1:
  12.5 69.5 all-gather.8
  84.2 41.0 all-gather.10
  127.4 52.1 all-gather.14
  217.0 28.5 all-gather.12
  248.1 53.6 all-gather.16
  311.0 24.0 reduce-scatter.4
  360.5 27.0 all-gather.18
  389.0 27.1 all-gather.20
  429.2 25.9 reduce-scatter.8
  457.5 25.9 reduce-scatter.6
  523.4 27.0 all-gather.22
  563.5 25.9 reduce-scatter.10
where the time goes:
time: 824 us; the launch traced here: 814 us
  waiting for transfers between devices  516 us (63%)
  matrix products  161 us (20%)
  other arithmetic  44.2 us (5%)
  blocking collectives  41.3 us (5%)
  local copies, waits for them, and re-layouts  27.1 us (3%)
  between operations  23.4 us (3%)
    unnamed x16, waiting for transfers between devices  296 us
    all_gather x2, waiting for transfers between devices, per_device(): lax.all_gather(normed_low, 'mlp', axis=0, tiled=True)  53.9 us
    reduce_scatter x2, waiting for transfers between devices, per_device(): lax.psum_scatter(slice_times(source=active, weight=w_down[layer_at]).asty...  50.6 us
    psum x1, blocking collectives, per_device(): square_sum = lax.psum(jnp.sum(own_grads * own_grads), ('seq', 'mlp'))  41.3 us
    reduce_scatter x2, waiting for transfers between devices, per_device(): lax.psum_scatter(slice_times_back(source=grad_before, weight=w_up[layer_a...  41.2 us
    dot_general x2, matrix products, rows_times(): return jnp.dot(piece_rows, weight, preferred_element_type=jnp.float32)  38.1 us
    all_gather x1, waiting for transfers between devices, per_device(): lax.all_gather(down_weight, 'seq', axis=2, tiled=True)  37 us
    all_gather x2, waiting for transfers between devices, per_device(): lax.all_gather(grad_low, 'mlp', axis=0, tiled=True)  36.5 us
  transfers between devices with their start and end apart: 14, of which 11 were waited for; matrix products, arithmetic and copies ran while one was open for 10% of the time, Pallas kernels for 0%

commit v1 on v0

v1 whole, which is shorter than its diff:
```python
import math
from functools import partial

import jax
import jax.numpy as jnp
from jax import lax
from jax.sharding import Mesh
from jax.sharding import PartitionSpec as P

HEADS = 12
HEAD_DIM = 64
ADAM_STEP = 2

ln_eps = 1e-06
masked_score = -1e30
clip_ratio = 0.05
adam_eps = 1e-08
decay_rate = 0.1
highest = lax.Precision.HIGHEST
ALL = ("z", "x", "core", "y")
f32 = jnp.float32
bf16 = jnp.bfloat16


def layer_norm(values, gain_row):
    center = values - jnp.mean(values, axis=-1, keepdims=True)
    spread = jnp.mean(center * center, axis=-1, keepdims=True)
    return center * lax.rsqrt(spread + ln_eps) * gain_row


def exact_gelu(values):
    return jax.nn.gelu(values, approximate=False)


def flip(value, axis):
    return lax.ppermute(value, axis, [(0, 1), (1, 0)])


def spread_over(value, axis):
    if lax.axis_size(axis) != 2:
        return lax.all_gather(value, axis)
    other = flip(value, axis)
    first = lax.axis_index(axis) == 0
    return jnp.stack([jnp.where(first, value, other), jnp.where(first, other, value)])


def ring_z(value):
    size = lax.axis_size("z")
    if size != 4:
        return lax.all_gather(value, "z")
    parts = [value]
    for step in range(1, size):
        parts.append(lax.ppermute(value, "z", [(i, (i + step) % size) for i in range(size)]))
    at = lax.axis_index("z")
    return jnp.stack(
        [lax.select_n((at - i) % size, *parts) for i in range(size)]
    )


def gather_group(part_a, part_b, first):
    width = part_a.shape[1]
    both = jnp.concatenate([part_a, part_b], axis=1)
    along = ring_z(both) if first else lax.all_gather(both, "z")
    a, b = along[:, :, :width], along[:, :, width:]
    a = spread_over(a, "x")
    b = spread_over(b, "y")
    a = spread_over(a, "y")
    b = spread_over(b, "x")
    a = spread_over(a, "core")
    b = spread_over(b, "core")
    return a.transpose(3, 2, 0, 4, 1, 5), b.transpose(3, 1, 0, 4, 2, 5)


def rows_of(gathered):
    z, x, core, rows, y, width = gathered.shape
    return gathered.reshape(z * x * core * rows, y, width)


def masked_scores(query_heads, key_heads, segments):
    raw_scores = jnp.einsum(
        "qhd,khd->hqk", query_heads, key_heads, preferred_element_type=f32
    ) * HEAD_DIM ** (-0.5)
    allowed = (segments[:, None] == segments[None, :])[None]
    return jnp.where(allowed, raw_scores, masked_score)


def attend_forward(query_heads, key_heads, value_heads, segments):
    scores = masked_scores(query_heads, key_heads, segments)
    row_max = jnp.max(scores, axis=2, keepdims=True)
    exponent = jnp.exp(scores - row_max)
    row_total = jnp.sum(exponent, axis=2, keepdims=True)
    attn_probs = (exponent / row_total).astype(bf16)
    mixed = jnp.einsum("hqk,khd->qhd", attn_probs, value_heads, preferred_element_type=f32)
    return mixed.astype(bf16).reshape(mixed.shape[0], -1), row_max + jnp.log(row_total)


def attend_backward(query_heads, key_heads, value_heads, segments, lse, grad_rows):
    scale = HEAD_DIM ** (-0.5)
    scores = masked_scores(query_heads, key_heads, segments)
    attn_probs = jnp.exp(scores - lse)
    grad_probs = jnp.einsum("qhd,khd->hqk", grad_rows, value_heads, preferred_element_type=f32)
    inner_sum = jnp.sum(attn_probs * grad_probs, axis=2, keepdims=True)
    grad_scores = (attn_probs * (grad_probs - inner_sum)).astype(bf16)
    grad_query = (
        jnp.einsum("hqk,khd->qhd", grad_scores, key_heads, preferred_element_type=f32) * scale
    )
    grad_keys = (
        jnp.einsum("hqk,qhd->khd", grad_scores, query_heads, preferred_element_type=f32) * scale
    )
    grad_values = jnp.einsum(
        "hqk,qhd->khd", attn_probs.astype(bf16), grad_rows, preferred_element_type=f32
    )
    tokens = grad_query.shape[0]
    return jnp.concatenate(
        [v.astype(bf16).reshape(tokens, -1) for v in (grad_query, grad_keys, grad_values)], axis=1
    )


def total_over(value):
    if lax.axis_size("z") != 4 or lax.axis_size("y") != 2:
        return lax.psum(value, ALL)
    core = lax.axis_index("core")
    low = value.astype(bf16)
    mine = jnp.where(core == 0, value[0], value[1])
    theirs = jnp.where(core == 0, low[1], low[0])
    total = mine + flip(theirs, "core").astype(f32)
    for axis in ("x", "y"):
        total = total + flip(total.astype(bf16), axis).astype(f32)
    for pairs in ([(0, 1), (1, 0), (2, 3), (3, 2)], [(0, 2), (2, 0), (1, 3), (3, 1)]):
        total = total + lax.ppermute(total.astype(bf16), "z", pairs).astype(f32)
    other = flip(total.astype(bf16), "core").astype(f32)
    return jnp.stack([jnp.where(core == 0, total, other), jnp.where(core == 0, other, total)])


def per_device(
    patches,
    segments,
    prompt_slots,
    norm_gains,
    qkv_weight,
    out_weight,
    up_weight,
    down_weight,
    cotangent,
    prompts,
    first_moment,
    second_moment,
    adam_betas,
    learn_rate,
):
    layers, _, width = norm_gains.shape
    tokens = patches.shape[0]
    y_size, y_at = lax.axis_size("y"), lax.axis_index("y")
    devices = y_size * lax.axis_size("z") * lax.axis_size("x") * lax.axis_size("core")
    rows = qkv_weight.shape[1]
    total_prompts = prompts.shape[0] * devices

    across = prompts.shape[0] // rows
    rides = across * rows == prompts.shape[0]
    if rides:
        shaped = prompts.reshape(rows, across)
        high_half = shaped.astype(bf16)
        low_half = (shaped - high_half.astype(f32)).astype(bf16)
        rider = jnp.concatenate([high_half, low_half], axis=1)
        rider = jnp.pad(rider, ((0, 0), (0, -rider.shape[1] % 128)))

    weights = []
    prompt_table = None
    if not rides:
        prompt_table = lax.all_gather(prompts, ALL).reshape(layers, -1, width)
    for layer_at in range(layers):
        cut = qkv_weight.shape[2] // y_size
        out_cut = width // y_size
        qkv_part = lax.dynamic_slice(qkv_weight[layer_at], (0, y_at * cut), (rows, cut))
        out_part = lax.dynamic_slice(out_weight[layer_at], (0, y_at * out_cut), (rows, out_cut))
        half = (cut + out_cut) // 2
        part_a = qkv_part[:, :half]
        part_b = jnp.concatenate([qkv_part[:, half:], out_part], axis=1)
        if layer_at == 0 and rides:
            part_a = jnp.concatenate([part_a, rider], axis=1)
        attn_a, attn_b = gather_group(part_a, part_b, layer_at == 0)
        if layer_at == 0 and rides:
            riders = attn_a[..., half:]
            riders = riders.transpose(0, 1, 2, 4, 3, 5)
            table = riders[..., :across].astype(f32) + riders[..., across : 2 * across].astype(f32)
            prompt_table = table.reshape(layers, -1, width)
        attn_a, attn_b = rows_of(attn_a[..., :half]), rows_of(attn_b)
        w_qkv = jnp.concatenate([attn_a, attn_b[..., : cut - half]], axis=2).reshape(width, -1)
        w_out = attn_b[..., cut - half :].reshape(width, -1)
        w_up, w_down = gather_group(up_weight[layer_at], down_weight[layer_at].T, False)
        w_up = rows_of(w_up).reshape(width, -1)
        w_down = rows_of(w_down).reshape(width, -1)
        weights.append((w_qkv, w_out, w_up, w_down))

    slot_total = prompt_table.shape[1]
    onehot = (prompt_slots[:, None] == jnp.arange(slot_total)[None, :]).astype(f32)
    is_prompt = (prompt_slots < slot_total)[:, None]
    hidden = patches.astype(f32)
    kept_state = []
    for layer_at in range(layers):
        w_qkv, w_out, w_up, w_down = weights[layer_at]
        inject = jnp.dot(onehot, prompt_table[layer_at], precision=highest)
        entry_rows = jnp.where(is_prompt, inject, hidden)
        normed_one, norm_one_back = jax.vjp(
            partial(layer_norm, gain_row=norm_gains[layer_at, 0]), entry_rows
        )
        qkv = jnp.dot(normed_one.astype(bf16), w_qkv, preferred_element_type=f32).astype(bf16)
        heads = [
            qkv[:, i * width : (i + 1) * width].reshape(tokens, HEADS, HEAD_DIM) for i in range(3)
        ]
        mixed_rows, lse = attend_forward(*heads, segments)
        middle = entry_rows + jnp.dot(mixed_rows, w_out, preferred_element_type=f32)
        normed_two, norm_two_back = jax.vjp(
            partial(layer_norm, gain_row=norm_gains[layer_at, 1]), middle
        )
        before = jnp.dot(normed_two.astype(bf16), w_up, preferred_element_type=f32)
        active = exact_gelu(before).astype(bf16)
        hidden = middle + jnp.einsum("tf,df->td", active, w_down, preferred_element_type=f32)
        kept_state.append((heads, lse, norm_one_back, norm_two_back, before))
    block_output = hidden.astype(bf16)
    gradient = cotangent.astype(f32)
    layer_grads = []
    for layer_at in reversed(range(layers)):
        w_qkv, w_out, w_up, w_down = weights[layer_at]
        heads, lse, norm_one_back, norm_two_back, before = kept_state[layer_at]
        grad_active = jnp.dot(gradient.astype(bf16), w_down, preferred_element_type=f32)
        grad_before = jax.vjp(exact_gelu, before)[1](grad_active)[0].astype(bf16)
        grad_normtwo = jnp.einsum("tf,df->td", grad_before, w_up, preferred_element_type=f32)
        grad_middle = gradient + norm_two_back(grad_normtwo)[0]
        grad_mixed = jnp.einsum(
            "te,de->td", grad_middle.astype(bf16), w_out, preferred_element_type=f32
        ).astype(bf16)
        grad_qkv = attend_backward(
            *heads, segments, lse, grad_mixed.reshape(tokens, HEADS, HEAD_DIM)
        )
        grad_normone = jnp.einsum("tc,dc->td", grad_qkv, w_qkv, preferred_element_type=f32)
        grad_entry = grad_middle + norm_one_back(grad_normone)[0]
        layer_grads.append(jnp.einsum("tp,td->pd", onehot, grad_entry, precision=highest))
        gradient = jnp.where(is_prompt, 0.0, grad_entry)

    prompt_grad = total_over(jnp.stack(layer_grads[::-1]))
    grad_norm = jnp.sqrt(jnp.sum(prompt_grad * prompt_grad))
    clip_limit = clip_ratio * math.sqrt(total_prompts)
    own_grads = lax.dynamic_slice(
        prompt_grad.reshape(-1), (lax.axis_index(ALL) * prompts.shape[0],), prompts.shape
    )
    clipped = own_grads * jnp.minimum(1.0, clip_limit / (grad_norm + 1e-06))
    beta_one = adam_betas[0]
    beta_two = adam_betas[1]
    step_value = float(ADAM_STEP)
    new_first = beta_one * first_moment + (1.0 - beta_one) * clipped
    new_second = beta_two * second_moment + (1.0 - beta_two) * clipped * clipped
    first_hat = new_first / (1.0 - beta_one**step_value)
    second_hat = new_second / (1.0 - beta_two**step_value)
    new_prompts = prompts - learn_rate[0] * (
        first_hat / (jnp.sqrt(second_hat) + adam_eps) + decay_rate * prompts
    )
    return (block_output, gradient, new_prompts, new_first, new_second, grad_norm.reshape(1))


def solution(mesh):
    seq_size, mlp_size = mesh.shape["seq"], mesh.shape["mlp"]
    grid = Mesh(mesh.devices.reshape(seq_size // 4, 2, 2, mlp_size), ALL)
    seq, mlp = ("z", "x", "core"), "y"
    in_specs = (
        P(ALL, None),
        P(ALL),
        P(ALL),
        P(),
        P(None, seq, None),
        P(None, seq, None),
        P(None, seq, mlp),
        P(None, mlp, seq),
        P(ALL, None),
        P(ALL),
        P(ALL),
        P(ALL),
        P(),
        P(),
    )
    out_specs = (P(ALL, None), P(ALL, None), P(ALL), P(ALL), P(ALL), P())
    return jax.shard_map(
        per_device, mesh=grid, in_specs=in_specs, out_specs=out_specs, check_vma=False
    )
```

time: 824 us -> 522 us (0.63)
  waiting for transfers between devices: 516 us -> 35.2 us
  local copies, waits for them, and re-layouts: 27.1 us -> 129 us
  other arithmetic: 44.2 us -> 89.7 us
  starting transfers between devices: 1.59 us -> 37 us
    unnamed x16 -> x2, waiting for transfers between devices: 296 us -> 0.03 us
    all_gather x8 -> x2, waiting for transfers between devices: 127 us -> 0.01 us  [gather_group(): along = ring_z(both) if first else lax.all_gather(both, 'z')]
    reduce_scatter x4 -> x0, waiting for transfers between devices: 91.8 us -> none  [the longest x2 50.6 us: per_device(): lax.psum_scatter(slice_times(source=active, weight=w_down[layer_at]).asty...]
    all_gather x0 -> x1, blocking collectives: none -> 43.2 us  [gather_group(): along = ring_z(both) if first else lax.all_gather(both, 'z')]
    psum x1 -> x0, blocking collectives: 41.3 us -> none  [per_device(): square_sum = lax.psum(jnp.sum(own_grads * own_grads), ('seq', 'mlp'))]
    transpose x0 -> x9, local copies, waits for them, and re-layouts: none -> 39.3 us  [the longest x7 38.2 us: gather_group(): return (a.transpose(3, 2, 0, 4, 1, 5), b.transpose(3, 1, 0, 4, 2, 5))]
    another operation x1 -> x39, other arithmetic: 0.04 us -> 37.2 us  [the longest x34 36.1 us: spread_over(): jnp.stack([jnp.where(first, value, other), jnp.where(first, other, value)])]
    ppermute x0 -> x33, starting transfers between devices: none -> 36.9 us  [the longest x28 30.2 us: flip(): return lax.ppermute(value, axis, [(0, 1), (1, 0)])]
  transfers between devices with their start and end apart: 14 -> 35, of which waited for: 11 -> 11; matrix products, arithmetic and copies ran while one was open for 10% -> 31% of each run, Pallas kernels for 0% -> 0%
where the time goes in v1:
time: 522 us; the launch traced here: 513 us
  matrix products  156 us (30%)
  local copies, waits for them, and re-layouts  129 us (25%)
  other arithmetic  89.7 us (17%)
  blocking collectives  43.2 us (8%)
  starting transfers between devices  37 us (7%)
  waiting for transfers between devices  35.2 us (7%)
  between operations  22.6 us (4%)
    all_gather x1, blocking collectives, gather_group(): along = ring_z(both) if first else lax.all_gather(both, 'z')  43.2 us
    unnamed x232, local copies, waits for them, and re-layouts  41.5 us
    transpose x7, local copies, waits for them, and re-layouts, gather_group(): return (a.transpose(3, 2, 0, 4, 1, 5), b.transpose(3, 1, 0, 4, 2, 5))  38.2 us
    dot_general x2, matrix products, per_device(): before = jnp.dot(normed_two.astype(bf16), w_up, preferred_element_type=f32)  36.8 us
    another operation x34, other arithmetic, spread_over(): jnp.stack([jnp.where(first, value, other), jnp.where(first, other, value)])  36.1 us
    ppermute x28, waiting for transfers between devices, flip(): return lax.ppermute(value, axis, [(0, 1), (1, 0)])  35.2 us
    ppermute x28, starting transfers between devices, flip(): return lax.ppermute(value, axis, [(0, 1), (1, 0)])  30.2 us
    dot_general x2, matrix products, per_device(): jnp.einsum('tf,df->td', grad_before, w_up, preferred_element_type=f32)  28.9 us
  transfers between devices with their start and end apart: 35, of which 11 were waited for; matrix products, arithmetic and copies ran while one was open for 31% of the time, Pallas kernels for 0%

profile of v1, /device:TPU:1, one launch (start us, length us, event | category | flops | bytes accessed | tf_op | source)
XLA Modules:
  0.0 512.8 jit_solution(11243665515793724814)
XLA Ops:
  12.1 3.2 collective-permute-start.1
  16.9 43.2 %all-gather.1 = bf16[192,1536]{1,0:T(8,128)(2,1)S(1)} all-gather(bf16[48,1536]{1,0:T(8,128)(2,1)S(1)} %pad_maximum_fusion.24), channel_id=3, replica_groups=mesh['z'=4,'x'=2,'core'=2,'y'=2] {'z'}, dimensions={0}, use_global_device_ids=true | all-gather | bytes 737280 | tf_op jit(solution)/shard_map/all_gather | solution.py:63
  71.1 3.3 collective-permute-done.6
  76.5 10.6 %collective-permute-done.16 = bf16[2,4,48,768]{3,2,1,0:T(8,128)(2,1)S(1)} collective-permute-done((bf16[2,4,48,768]{3,2,1,0:T(8,128)(2,1)S(1)}, bf16[2,4,48,768]{3,2,1,0:T(8,128)(2,1)S(1)}, u32[]{:S(2)}, u32[]{:S(2)}) %collective-permute-start.16) | collective-permute-done | bytes 589856 | tf_op jit(solution)/shard_map/ppermute | solution.py:36
  88.3 6.7 %collective-permute-start.17 = (bf16[2,2,4,48,768]{4,3,2,1,0:T(8,128)(2,1)}, bf16[2,2,4,48,768]{4,3,2,1,0:T(8,128)(2,1)}, u32[]{:S(2)}, u32[]{:S(2)}) collective-permute-start(bf16[2,2,4,48,768]{4,3,2,1,0:T(8,128)(2,1)} %pad_maximum_fusion.10), channel_id=1, source_target_pairs={{0,2},{2,0},{1,3},{3,1},{4,6},{6,4},{5,7},{7,5},{8,10},{10,8},{9,1... | collective-permute-start | bytes 3538952 | tf_op jit(solution)/shard_map/ppermute | solution.py:36
  95.0 5.3 %collective-permute-done.7 = bf16[2,4,48,768]{3,2,1,0:T(8,128)(2,1)S(1)} collective-permute-done((bf16[2,4,48,768]{3,2,1,0:T(8,128)(2,1)S(1)}, bf16[2,4,48,768]{3,2,1,0:T(8,128)(2,1)S(1)}, u32[]{:S(2)}, u32[]{:S(2)}) %collective-permute-start.7) | collective-permute-done | bytes 589856 | tf_op jit(solution)/shard_map/ppermute | solution.py:36
  131.1 3.4 pad_maximum_fusion.1
  134.4 5.9 %copy.98 = bf16[768,2,1152]{0,2,1:T(8,128)(2,1)} copy(bf16[768,2,1152]{2,0,1:T(8,128)(2,1)} %pad_maximum_fusion.1) | data formatting | bytes 7077888 | tf_op jit(solution)/shard_map/concatenate | solution.py:188
  157.8 6.0 %copy.88 = bf16[768,2,1152]{0,2,1:T(8,128)(2,1)} copy(bf16[768,2,1152]{2,0,1:T(8,128)(2,1)} %pad_maximum_fusion) | data formatting | bytes 7077888 | tf_op jit(solution)/shard_map/concatenate | solution.py:188
  182.1 4.7 fusion.64
  190.5 6.1 %collective-permute-done.13 = bf16[2,4,48,1536]{3,2,1,0:T(8,128)(2,1)} collective-permute-done((bf16[2,4,48,1536]{3,2,1,0:T(8,128)(2,1)}, bf16[2,4,48,1536]{3,2,1,0:T(8,128)(2,1)}, u32[]{:S(2)}, u32[]{:S(2)}) %collective-permute-start.13) | collective-permute-done | bytes 1179680 | tf_op jit(solution)/shard_map/ppermute | solution.py:36
  213.0 9.3 %copy.95 = bf16[4,2,2,48,2,1536]{5,4,3,2,1,0:T(2,128)(2,1)} copy(bf16[4,2,2,48,2,1536]{5,3,0,4,1,2:T(8,128)(2,1)} %maximum_bitcast_fusion.1) | data formatting | bytes 9437184 | tf_op jit(solution)/shard_map/transpose | solution.py:71
  222.3 5.8 %copy.125 = bf16[96,8,2,1536]{3,1,2,0:T(8,128)(2,1)} copy(bf16[96,8,2,1536]{3,2,1,0:T(2,128)(2,1)} %bitcast.287) | data formatting | bytes 9437184
  232.7 9.5 %copy.105 = bf16[4,2,2,48,2,1536]{5,4,3,2,1,0:T(2,128)(2,1)} copy(bf16[4,2,2,48,2,1536]{5,3,0,4,1,2:T(8,128)(2,1)} %maximum_bitcast_fusion.3) | data formatting | bytes 9437184 | tf_op jit(solution)/shard_map/transpose | solution.py:71
  242.2 5.8 %copy.127 = bf16[96,8,2,1536]{3,1,2,0:T(8,128)(2,1)} copy(bf16[96,8,2,1536]{3,2,1,0:T(2,128)(2,1)} %bitcast.288) | data formatting | bytes 9437184
  252.6 9.3 %copy.94 = bf16[4,2,2,48,2,1536]{5,4,3,2,1,0:T(2,128)(2,1)} copy(bf16[4,2,2,48,2,1536]{5,3,0,1,4,2:T(8,128)(2,1)} %maximum_bitcast_fusion) | data formatting | bytes 9437184 | tf_op jit(solution)/shard_map/transpose | solution.py:71
  261.9 6.0 %copy.124 = bf16[96,8,2,1536]{3,1,2,0:T(8,128)(2,1)} copy(bf16[96,8,2,1536]{3,2,1,0:T(2,128)(2,1)} %bitcast.289) | data formatting | bytes 9437184
  272.4 9.3 %copy.104 = bf16[4,2,2,48,2,1536]{5,4,3,2,1,0:T(2,128)(2,1)} copy(bf16[4,2,2,48,2,1536]{5,3,0,1,4,2:T(8,128)(2,1)} %maximum_bitcast_fusion.2) | data formatting | bytes 9437184 | tf_op jit(solution)/shard_map/transpose | solution.py:71
  281.8 5.9 %copy.126 = bf16[96,8,2,1536]{3,1,2,0:T(8,128)(2,1)} copy(bf16[96,8,2,1536]{3,2,1,0:T(2,128)(2,1)} %bitcast.290) | data formatting | bytes 9437184
  287.7 17.8 %fusion.4 = (f32[512,3072]{1,0:T(8,128)S(1)}, f32[512,3072]{1,0:T(8,128)S(1)}) fusion(bf16[768,3072]{1,0:T(8,128)(2,1)} %bitcast.311, f32[512,768]{1,0:T(8,128)S(1)} %get-tuple-element.122, f32[768]{0:T(1024)S(1)} %get-tuple-element.7, f32[512]{0:T(512)S(1)} %fusion.103, f32[512]{0:T(512)S(1)} %broadcast_multiply_fusion.2), kind=kOutput, calls=%fused_computation.18 | convolution fusion | flops 2515009536 | bytes 18881536 | tf_op jit(solution)/shard_map/dot_general | solution.py:216
  326.8 3.6 fusion.63
  331.7 19.0 %fusion.5 = (f32[512,3072]{1,0:T(8,128)}, f32[512,3072]{1,0:T(8,128)}) fusion(bf16[768,3072]{1,0:T(8,128)(2,1)} %bitcast.313, f32[512,768]{1,0:T(8,128)S(1)} %get-tuple-element.130, f32[768]{0:T(1024)S(1)} %copy-done.91, f32[512]{0:T(512)S(1)} %fusion.105, f32[512]{0:T(512)S(1)} %broadcast_multiply_fusion), kind=kOutput, calls=%fused_computation.19 | convolution fusion | flops 2515009536 | bytes 18881536 | tf_op jit(solution)/shard_map/dot_general | solution.py:216
  350.7 14.3 %multiply_reduce_fusion.5 = (f32[512]{0:T(512)S(1)}, f32[512,768]{1,0:T(8,128)}) fusion(f32[512,768]{1,0:T(8,128)S(1)} %get-tuple-element.130, f32[768]{0:T(1024)S(1)} %copy-done.91, f32[512]{0:T(512)S(1)} %broadcast_multiply_fusion, bf16[768,3072]{1,0:T(8,128)(2,1)} %bitcast.314, f32[512,3072]{1,0:T(8,128)} %get-tuple-element.131, ...), kind=kOutput, calls=%fused_computation.123 | convolution fusion | flops 4855430656 | bytes 25959424 | tf_op jit(solution)/shard_map/tf,df->td/dot_general | solution.py:228
  372.3 8.9 %fusion.57 = bf16[12,64,512]{2,1,0:T(8,128)(2,1)} fusion(bf16[512,12,64]{0,2,1:T(8,128)(2,1)} %bitcast.327, f32[12,512]{1,0:T(8,128)S(1)} %log_add_fusion.1, f32[12,512,512]{1,2,0:T(8,128)} %copy-done.1, pred[512,512]{0,1:T(8,128)(4,1)S(1)} %broadcast_compare_fusion), kind=kOutput, calls=%fused_computation.142 | convolution fusion | flops 415629312 | bytes 14442496 | tf_op jit(solution)/shard_map/hqk,qhd->khd/dot_general | solution.py:110
  381.3 9.6 %multiply_reduce_fusion.1 = (f32[12,512]{1,0:T(8,128)S(1)}, f32[12,512,512]{1,2,0:T(8,128)}) fusion(f32[12,512]{1,0:T(8,128)S(1)} %log_add_fusion.1, f32[12,512,512]{1,2,0:T(8,128)} %copy-done.1, pred[512,512]{0,1:T(8,128)(4,1)S(1)} %broadcast_compare_fusion, bf16[512,12,64]{0,2,1:T(8,128)(2,1)S(1)} %bitcast.328, bf16[512,12,64]{0,2,1:T(8,128)(2,1)S(1)} %bitcast.326), kind=kOutput, calls=%fused_computation.4 | convolution fusion | flops 418375680 | bytes 27049984 | tf_op jit(solution)/shard_map/qhd,khd->hqk/dot_general | solution.py:101
  390.9 7.2 %multiply_convert_fusion.1 = bf16[12,512,512]{1,2,0:T(8,128)(2,1)S(1)} fusion(f32[12,512,512]{1,2,0:T(8,128)} %get-tuple-element.136, f32[12,512]{1,0:T(8,128)S(1)} %get-tuple-element.135, f32[12,512]{1,0:T(8,128)S(1)} %log_add_fusion.1, f32[12,512,512]{1,2,0:T(8,128)S(1)} %bitcast.282, pred[512,512]{0,1:T(8,128)(4,1)S(1)} %broadcast_compare_fusion), kind=kLoop, calls=%fused_computation.3 | loop fusion | flops 18874368 | bytes 31768576 | tf_op jit(solution)/shard_map/convert_element_type | solution.py:103
  408.2 14.7 %multiply_reduce_fusion.3 = (f32[512]{0:T(512)S(1)}, f32[512,768]{1,0:T(8,128)}) fusion(f32[512,768]{1,0:T(8,128)S(1)} %get-tuple-element.122, f32[768]{0:T(1024)S(1)} %get-tuple-element.7, f32[512]{0:T(512)S(1)} %broadcast_multiply_fusion.2, bf16[768,3072]{1,0:T(8,128)(2,1)} %bitcast.312, f32[512,3072]{1,0:T(8,128)} %copy-done.7, ...), kind=kOutput, calls=%fused_computation.117 | convolution fusion | flops 4855823872 | bytes 26746368 | tf_op jit(solution)/shard_map/tf,df->td/dot_general | solution.py:228
  432.1 8.9 %fusion.60 = bf16[12,64,512]{2,1,0:T(8,128)(2,1)} fusion(bf16[512,12,64]{0,2,1:T(8,128)(2,1)} %bitcast.329, f32[12,512]{1,0:T(8,128)S(1)} %copy-done.81, f32[12,512,512]{1,2,0:T(8,128)} %copy-done, pred[512,512]{0,1:T(8,128)(4,1)S(1)} %broadcast_compare_fusion), kind=kOutput, calls=%fused_computation.143 | convolution fusion | flops 415629312 | bytes 14442496 | tf_op jit(solution)/shard_map/hqk,qhd->khd/dot_general | solution.py:110
  441.1 9.6 %multiply_reduce_fusion = (f32[12,512]{1,0:T(8,128)S(1)}, f32[12,512,512]{1,2,0:T(8,128)}) fusion(f32[12,512]{1,0:T(8,128)S(1)} %copy-done.81, f32[12,512,512]{1,2,0:T(8,128)} %copy-done, pred[512,512]{0,1:T(8,128)(4,1)S(1)} %broadcast_compare_fusion, bf16[512,12,64]{0,2,1:T(8,128)(2,1)S(1)} %bitcast.330, bf16[512,12,64]{0,2,1:T(8,128)(2,1)S(1)} %bitcast.324), kind=kOutput, calls=%fused_computation.1 | convolution fusion | flops 418375680 | bytes 27049984 | tf_op jit(solution)/shard_map/qhd,khd->hqk/dot_general | solution.py:101
  450.7 7.3 %multiply_convert_fusion = bf16[12,512,512]{1,2,0:T(8,128)(2,1)S(1)} fusion(f32[12,512,512]{1,2,0:T(8,128)} %get-tuple-element.142, f32[12,512]{1,0:T(8,128)S(1)} %get-tuple-element.141, f32[12,512]{1,0:T(8,128)S(1)} %copy-done.81, f32[12,512,512]{1,2,0:T(8,128)S(1)} %bitcast.280, pred[512,512]{0,1:T(8,128)(4,1)S(1)} %broadcast_compare_fusion), kind=kLoop, calls=%fused_computation | loop fusion | flops 18874368 | bytes 31768576 | tf_op jit(solution)/shard_map/convert_element_type | solution.py:103
  469.5 3.6 collective-permute-done.28
  486.0 9.5 %add_convert_fusion.2 = bf16[512,768]{1,0:T(8,128)(2,1)} fusion(f32[512,768]{1,0:T(8,128)S(1)} %get-tuple-element.130, bf16[768,3072]{1,0:T(8,128)(2,1)} %bitcast.292, f32[512,3072]{1,0:T(8,128)} %get-tuple-element.131, f32[512,3072]{1,0:T(8,128)} %get-tuple-element.132), kind=kOutput, calls=%fused_computation.124 | convolution fusion | flops 2421424128 | bytes 19660800 | tf_op jit(solution)/shard_map/tf,df->td/dot_general | solution.py:218
  (452 shorter events, 196.8 us)
Async XLA Ops:
  7.2 101.4 %all-gather.6.cloned.1.call-start = ((), (), s32[]{:S(2)}) async-start(), calls=%async_computation | async-start | bytes 1474560 | tf_op jit(solution)/shard_map/all_gather | solution.py:63
  10.0 102.0 %all-gather.8.cloned.1.call-start = ((), (), s32[]{:S(2)}) async-start(), calls=%async_computation.1 | async-start | bytes 1474560 | tf_op jit(solution)/shard_map/all_gather | solution.py:63
  12.1 52.8 %collective-permute-start.1 = (bf16[48,1664]{1,0:T(8,128)(2,1)S(1)}, bf16[48,1664]{1,0:T(8,128)(2,1)S(1)}, u32[]{:S(2)}, u32[]{:S(2)}) collective-permute-start(bf16[48,1664]{1,0:T(8,128)(2,1)S(1)} %pad_maximum_fusion.23), channel_id=1, source_target_pairs={{0,16},{8,24},{16,0},{24,8},{1,17},{9,25},{17,1},{25,9},{2,18},{10... | collective-permute-start | bytes 479240 | tf_op jit(solution)/shard_map/ppermute | solution.py:53
  15.3 49.6 %collective-permute-start.2 = (bf16[48,1664]{1,0:T(8,128)(2,1)S(1)}, bf16[48,1664]{1,0:T(8,128)(2,1)S(1)}, u32[]{:S(2)}, u32[]{:S(2)}) collective-permute-start(bf16[48,1664]{1,0:T(8,128)(2,1)S(1)} %pad_maximum_fusion.23), channel_id=1, source_target_pairs={{0,24},{8,0},{16,8},{24,16},{1,25},{9,1},{17,9},{25,17},{2,26},{10... | collective-permute-start | bytes 479240 | tf_op jit(solution)/shard_map/ppermute | solution.py:53
  16.4 48.6 %collective-permute-start = (bf16[48,1664]{1,0:T(8,128)(2,1)S(1)}, bf16[48,1664]{1,0:T(8,128)(2,1)S(1)}, u32[]{:S(2)}, u32[]{:S(2)}) collective-permute-start(bf16[48,1664]{1,0:T(8,128)(2,1)S(1)} %pad_maximum_fusion.23), channel_id=1, source_target_pairs={{0,8},{8,16},{16,24},{24,0},{1,9},{9,17},{17,25},{25,1},{2,10},{10... | collective-permute-start | bytes 479240 | tf_op jit(solution)/shard_map/ppermute | solution.py:53
  60.8 6.1 %collective-permute-start.15 = (bf16[4,48,768]{2,1,0:T(8,128)(2,1)}, bf16[4,48,768]{2,1,0:T(8,128)(2,1)S(1)}, u32[]{:S(2)}, u32[]{:S(2)}) collective-permute-start(bf16[4,48,768]{2,1,0:T(8,128)(2,1)} %get-tuple-element.99), channel_id=1, source_target_pairs={{0,4},{4,0},{1,5},{5,1},{2,6},{6,2},{3,7},{7,3},{8,12},{12,8},{9,1... | collective-permute-start | bytes 884744 | tf_op jit(solution)/shard_map/ppermute | solution.py:36
  62.0 5.9 %collective-permute-start.18 = (bf16[4,48,768]{2,1,0:T(8,128)(2,1)S(1)}, bf16[4,48,768]{2,1,0:T(8,128)(2,1)}, u32[]{:S(2)}, u32[]{:S(2)}) collective-permute-start(bf16[4,48,768]{2,1,0:T(8,128)(2,1)S(1)} %get-tuple-element.100), channel_id=1, source_target_pairs={{0,1},{1,0},{2,3},{3,2},{4,5},{5,4},{6,7},{7,6},{8,9},{9,8},{10,11... | collective-permute-start | bytes 884744 | tf_op jit(solution)/shard_map/ppermute | solution.py:36
  65.3 9.2 %collective-permute-start.6 = (bf16[4,48,768]{2,1,0:T(8,128)(2,1)S(1)}, bf16[4,48,768]{2,1,0:T(8,128)(2,1)S(1)}, u32[]{:S(2)}, u32[]{:S(2)}) collective-permute-start(bf16[4,48,768]{2,1,0:T(8,128)(2,1)S(1)} %pad_maximum_fusion.20), channel_id=1, source_target_pairs={{0,1},{1,0},{2,3},{3,2},{4,5},{5,4},{6,7},{7,6},{8,9},{9,8},{10,11... | collective-permute-start | bytes 884744 | tf_op jit(solution)/shard_map/ppermute | solution.py:36
  65.7 9.4 %collective-permute-start.3 = (bf16[4,48,896]{2,1,0:T(8,128)(2,1)S(1)}, bf16[4,48,896]{2,1,0:T(8,128)(2,1)S(1)}, u32[]{:S(2)}, u32[]{:S(2)}) collective-permute-start(bf16[4,48,896]{2,1,0:T(8,128)(2,1)S(1)} %slice.169), channel_id=1, source_target_pairs={{0,4},{4,0},{1,5},{5,1},{2,6},{6,2},{3,7},{7,3},{8,12},{12,8},{9,1... | collective-permute-start | bytes 1032200 | tf_op jit(solution)/shard_map/ppermute | solution.py:36
  69.1 25.9 %collective-permute-start.19 = (bf16[2,4,48,768]{3,2,1,0:T(8,128)(2,1)S(1)}, bf16[2,4,48,768]{3,2,1,0:T(8,128)(2,1)S(1)}, u32[]{:S(2)}, u32[]{:S(2)}) collective-permute-start(bf16[2,4,48,768]{3,2,1,0:T(8,128)(2,1)S(1)} %pad_maximum_fusion.18), channel_id=1, source_target_pairs={{0,4},{4,0},{1,5},{5,1},{2,6},{6,2},{3,7},{7,3},{8,12},{12,8},{9,1... | collective-permute-start | bytes 1769480 | tf_op jit(solution)/shard_map/ppermute | solution.py:36
  69.8 17.3 %collective-permute-start.16 = (bf16[2,4,48,768]{3,2,1,0:T(8,128)(2,1)S(1)}, bf16[2,4,48,768]{3,2,1,0:T(8,128)(2,1)S(1)}, u32[]{:S(2)}, u32[]{:S(2)}) collective-permute-start(bf16[2,4,48,768]{3,2,1,0:T(8,128)(2,1)S(1)} %pad_maximum_fusion.17), channel_id=1, source_target_pairs={{0,1},{1,0},{2,3},{3,2},{4,5},{5,4},{6,7},{7,6},{8,9},{9,8},{10,11... | collective-permute-start | bytes 1769480 | tf_op jit(solution)/shard_map/ppermute | solution.py:36
  74.6 25.6 %collective-permute-start.7 = (bf16[2,4,48,768]{3,2,1,0:T(8,128)(2,1)S(1)}, bf16[2,4,48,768]{3,2,1,0:T(8,128)(2,1)S(1)}, u32[]{:S(2)}, u32[]{:S(2)}) collective-permute-start(bf16[2,4,48,768]{3,2,1,0:T(8,128)(2,1)S(1)} %pad_maximum_fusion.16), channel_id=1, source_target_pairs={{0,4},{4,0},{1,5},{5,1},{2,6},{6,2},{3,7},{7,3},{8,12},{12,8},{9,1... | collective-permute-start | bytes 1769480 | tf_op jit(solution)/shard_map/ppermute | solution.py:36
  75.3 30.5 %collective-permute-start.4 = (bf16[2,4,48,896]{3,2,0,1:T(8,128)(2,1)S(1)}, bf16[2,4,48,896]{3,2,0,1:T(8,128)(2,1)S(1)}, u32[]{:S(2)}, u32[]{:S(2)}) collective-permute-start(bf16[2,4,48,896]{3,2,0,1:T(8,128)(2,1)S(1)} %pad_maximum_fusion.14), channel_id=1, source_target_pairs={{0,1},{1,0},{2,3},{3,2},{4,5},{5,4},{6,7},{7,6},{8,9},{9,8},{10,11... | collective-permute-start | bytes 2064392 | tf_op jit(solution)/shard_map/ppermute | solution.py:36
  88.3 26.1 %collective-permute-start.17 = (bf16[2,2,4,48,768]{4,3,2,1,0:T(8,128)(2,1)}, bf16[2,2,4,48,768]{4,3,2,1,0:T(8,128)(2,1)}, u32[]{:S(2)}, u32[]{:S(2)}) collective-permute-start(bf16[2,2,4,48,768]{4,3,2,1,0:T(8,128)(2,1)} %pad_maximum_fusion.10), channel_id=1, source_target_pairs={{0,2},{2,0},{1,3},{3,1},{4,6},{6,4},{5,7},{7,5},{8,10},{10,8},{9,1... | collective-permute-start | bytes 3538952 | tf_op jit(solution)/shard_map/ppermute | solution.py:36
  101.8 15.8 %collective-permute-start.8 = (bf16[2,2,4,48,768]{4,3,2,1,0:T(8,128)(2,1)}, bf16[2,2,4,48,768]{4,3,2,1,0:T(8,128)(2,1)}, u32[]{:S(2)}, u32[]{:S(2)}) collective-permute-start(bf16[2,2,4,48,768]{4,3,2,1,0:T(8,128)(2,1)} %pad_maximum_fusion.7), channel_id=1, source_target_pairs={{0,2},{2,0},{1,3},{3,1},{4,6},{6,4},{5,7},{7,5},{8,10},{10,8},{9,1... | collective-permute-start | bytes 3538952 | tf_op jit(solution)/shard_map/ppermute | solution.py:36
  105.7 18.8 %collective-permute-start.20 = (bf16[2,2,4,48,768]{4,3,2,1,0:T(8,128)(2,1)}, bf16[2,2,4,48,768]{4,3,2,1,0:T(8,128)(2,1)}, u32[]{:S(2)}, u32[]{:S(2)}) collective-permute-start(bf16[2,2,4,48,768]{4,3,2,1,0:T(8,128)(2,1)} %pad_maximum_fusion.11), channel_id=1, source_target_pairs={{0,2},{2,0},{1,3},{3,1},{4,6},{6,4},{5,7},{7,5},{8,10},{10,8},{9,1... | collective-permute-start | bytes 3538952 | tf_op jit(solution)/shard_map/ppermute | solution.py:36
  108.0 44.5 %collective-permute-start.5 = (bf16[2,2,4,48,896]{4,3,1,2,0:T(8,128)(2,1)}, bf16[2,2,4,48,896]{4,3,1,2,0:T(8,128)(2,1)}, u32[]{:S(2)}, u32[]{:S(2)}) collective-permute-start(bf16[2,2,4,48,896]{4,3,1,2,0:T(8,128)(2,1)} %pad_maximum_fusion.6), channel_id=1, source_target_pairs={{0,2},{2,0},{1,3},{3,1},{4,6},{6,4},{5,7},{7,5},{8,10},{10,8},{9,1... | collective-permute-start | bytes 4128776 | tf_op jit(solution)/shard_map/ppermute | solution.py:36
  110.9 36.3 %collective-permute-start.9 = (bf16[4,48,1536]{2,1,0:T(8,128)(2,1)}, bf16[4,48,1536]{2,1,0:T(8,128)(2,1)}, u32[]{:S(2)}, u32[]{:S(2)}) collective-permute-start(bf16[4,48,1536]{2,1,0:T(8,128)(2,1)} %get-tuple-element.81), channel_id=1, source_target_pairs={{0,4},{4,0},{1,5},{5,1},{2,6},{6,2},{3,7},{7,3},{8,12},{12,8},{9,1... | collective-permute-start | bytes 1769480 | tf_op jit(solution)/shard_map/ppermute | solution.py:36
  114.4 32.8 %collective-permute-start.12 = (bf16[4,48,1536]{2,1,0:T(8,128)(2,1)}, bf16[4,48,1536]{2,1,0:T(8,128)(2,1)}, u32[]{:S(2)}, u32[]{:S(2)}) collective-permute-start(bf16[4,48,1536]{2,1,0:T(8,128)(2,1)} %get-tuple-element.82), channel_id=1, source_target_pairs={{0,1},{1,0},{2,3},{3,2},{4,5},{5,4},{6,7},{7,6},{8,9},{9,8},{10,11... | collective-permute-start | bytes 1769480 | tf_op jit(solution)/shard_map/ppermute | solution.py:36
  117.6 22.8 %collective-permute-start.21 = (bf16[4,48,1536]{2,1,0:T(8,128)(2,1)}, bf16[4,48,1536]{2,1,0:T(8,128)(2,1)}, u32[]{:S(2)}, u32[]{:S(2)}) collective-permute-start(bf16[4,48,1536]{2,1,0:T(8,128)(2,1)} %get-tuple-element.73), channel_id=1, source_target_pairs={{0,4},{4,0},{1,5},{5,1},{2,6},{6,2},{3,7},{7,3},{8,12},{12,8},{9,1... | collective-permute-start | bytes 1769480 | tf_op jit(solution)/shard_map/ppermute | solution.py:36
  124.5 17.5 %collective-permute-start.24 = (bf16[4,48,1536]{2,1,0:T(8,128)(2,1)}, bf16[4,48,1536]{2,1,0:T(8,128)(2,1)}, u32[]{:S(2)}, u32[]{:S(2)}) collective-permute-start(bf16[4,48,1536]{2,1,0:T(8,128)(2,1)} %get-tuple-element.74), channel_id=1, source_target_pairs={{0,1},{1,0},{2,3},{3,2},{4,5},{5,4},{6,7},{7,6},{8,9},{9,8},{10,11... | collective-permute-start | bytes 1769480 | tf_op jit(solution)/shard_map/ppermute | solution.py:36
  144.6 45.9 %collective-permute-start.25 = (bf16[2,4,48,1536]{3,2,1,0:T(8,128)(2,1)}, bf16[2,4,48,1536]{3,2,1,0:T(8,128)(2,1)}, u32[]{:S(2)}, u32[]{:S(2)}) collective-permute-start(bf16[2,4,48,1536]{3,2,1,0:T(8,128)(2,1)} %pad_maximum_fusion.13), channel_id=1, source_target_pairs={{0,4},{4,0},{1,5},{5,1},{2,6},{6,2},{3,7},{7,3},{8,12},{12,8},{9,1... | collective-permute-start | bytes 3538952 | tf_op jit(solution)/shard_map/ppermute | solution.py:36
  146.0 57.7 %collective-permute-start.22 = (bf16[2,4,48,1536]{3,2,1,0:T(8,128)(2,1)}, bf16[2,4,48,1536]{3,2,1,0:T(8,128)(2,1)}, u32[]{:S(2)}, u32[]{:S(2)}) collective-permute-start(bf16[2,4,48,1536]{3,2,1,0:T(8,128)(2,1)} %pad_maximum_fusion.12), channel_id=1, source_target_pairs={{0,1},{1,0},{2,3},{3,2},{4,5},{5,4},{6,7},{7,6},{8,9},{9,8},{10,11... | collective-permute-start | bytes 3538952 | tf_op jit(solution)/shard_map/ppermute | solution.py:36
  149.9 46.6 %collective-permute-start.13 = (bf16[2,4,48,1536]{3,2,1,0:T(8,128)(2,1)}, bf16[2,4,48,1536]{3,2,1,0:T(8,128)(2,1)}, u32[]{:S(2)}, u32[]{:S(2)}) collective-permute-start(bf16[2,4,48,1536]{3,2,1,0:T(8,128)(2,1)} %pad_maximum_fusion.9), channel_id=1, source_target_pairs={{0,4},{4,0},{1,5},{5,1},{2,6},{6,2},{3,7},{7,3},{8,12},{12,8},{9,1... | collective-permute-start | bytes 3538952 | tf_op jit(solution)/shard_map/ppermute | solution.py:36
  152.3 51.4 %collective-permute-start.10 = (bf16[2,4,48,1536]{3,2,1,0:T(8,128)(2,1)}, bf16[2,4,48,1536]{3,2,1,0:T(8,128)(2,1)}, u32[]{:S(2)}, u32[]{:S(2)}) collective-permute-start(bf16[2,4,48,1536]{3,2,1,0:T(8,128)(2,1)} %pad_maximum_fusion.8), channel_id=1, source_target_pairs={{0,1},{1,0},{2,3},{3,2},{4,5},{5,4},{6,7},{7,6},{8,9},{9,8},{10,11... | collective-permute-start | bytes 3538952 | tf_op jit(solution)/shard_map/ppermute | solution.py:36
  199.0 11.2 %collective-permute-start.14 = (bf16[2,2,4,48,1536]{4,3,2,1,0:T(8,128)(2,1)S(1)}, bf16[2,2,4,48,1536]{4,3,2,1,0:T(8,128)(2,1)S(1)}, u32[]{:S(2)}, u32[]{:S(2)}) collective-permute-start(bf16[2,2,4,48,1536]{4,3,2,1,0:T(8,128)(2,1)S(1)} %pad_maximum_fusion.3), channel_id=1, source_target_pairs={{0,2},{2,0},{1,3},{3,1},{4,6},{6,4},{5,7},{7,5},{8,10},{10,8},{9,1... | collective-permute-start | bytes 7077896 | tf_op jit(solution)/shard_map/ppermute | solution.py:36
  203.7 24.5 %collective-permute-start.26 = (bf16[2,2,4,48,1536]{4,3,2,1,0:T(8,128)(2,1)}, bf16[2,2,4,48,1536]{4,3,2,1,0:T(8,128)(2,1)}, u32[]{:S(2)}, u32[]{:S(2)}) collective-permute-start(bf16[2,2,4,48,1536]{4,3,2,1,0:T(8,128)(2,1)} %pad_maximum_fusion.5), channel_id=1, source_target_pairs={{0,2},{2,0},{1,3},{3,1},{4,6},{6,4},{5,7},{7,5},{8,10},{10,8},{9,1... | collective-permute-start | bytes 7077896 | tf_op jit(solution)/shard_map/ppermute | solution.py:36
  207.7 40.3 %collective-permute-start.11 = (bf16[2,2,4,48,1536]{4,3,2,1,0:T(8,128)(2,1)}, bf16[2,2,4,48,1536]{4,3,2,1,0:T(8,128)(2,1)}, u32[]{:S(2)}, u32[]{:S(2)}) collective-permute-start(bf16[2,2,4,48,1536]{4,3,2,1,0:T(8,128)(2,1)} %pad_maximum_fusion.2), channel_id=1, source_target_pairs={{0,2},{2,0},{1,3},{3,1},{4,6},{6,4},{5,7},{7,5},{8,10},{10,8},{9,1... | collective-permute-start | bytes 7077896 | tf_op jit(solution)/shard_map/ppermute | solution.py:36
  209.8 58.1 %collective-permute-start.23 = (bf16[2,2,4,48,1536]{4,3,2,1,0:T(8,128)(2,1)}, bf16[2,2,4,48,1536]{4,3,2,1,0:T(8,128)(2,1)}, u32[]{:S(2)}, u32[]{:S(2)}) collective-permute-start(bf16[2,2,4,48,1536]{4,3,2,1,0:T(8,128)(2,1)} %pad_maximum_fusion.4), channel_id=1, source_target_pairs={{0,2},{2,0},{1,3},{3,1},{4,6},{6,4},{5,7},{7,5},{8,10},{10,8},{9,1... | collective-permute-start | bytes 7077896 | tf_op jit(solution)/shard_map/ppermute | solution.py:36
  477.9 6.5 %collective-permute-start.30 = (bf16[50,768]{1,0:T(8,128)(2,1)}, bf16[50,768]{1,0:T(8,128)(2,1)}, u32[]{:S(2)}, u32[]{:S(2)}) collective-permute-start(bf16[50,768]{1,0:T(8,128)(2,1)} %fusion.126), channel_id=1, source_target_pairs={{0,8},{8,0},{16,24},{24,16},{1,9},{9,1},{17,25},{25,17},{2,10},{10... | collective-permute-start | bytes 230408 | tf_op jit(solution)/shard_map/ppermute | solution.py:130
  485.4 10.2 %collective-permute-start.31 = (bf16[50,768]{1,0:T(8,128)(2,1)S(1)}, bf16[50,768]{1,0:T(8,128)(2,1)S(1)}, u32[]{:S(2)}, u32[]{:S(2)}) collective-permute-start(bf16[50,768]{1,0:T(8,128)(2,1)S(1)} %fusion.97), channel_id=1, source_target_pairs={{0,16},{16,0},{8,24},{24,8},{1,17},{17,1},{9,25},{25,9},{2,18},{18... | collective-permute-start | bytes 230408 | tf_op jit(solution)/shard_map/ppermute | solution.py:130
  496.6 4.3 collective-permute-start.32
  (117 other events, 971.6 us)
Sparse Core Ops, SparseCore 0:
  10.2 44.6 all-gather.5
  64.1 28.9 all-gather.7

commit v2 on v1

v2 whole, which is shorter than its diff:
```python
import math
from functools import partial

import jax
import jax.numpy as jnp
from jax import lax
from jax.experimental import pallas as pl
from jax.experimental.pallas import tpu as pltpu
from jax.sharding import Mesh
from jax.sharding import PartitionSpec as P

HEADS = 12
HEAD_DIM = 64
ADAM_STEP = 2

ln_eps = 1e-06
masked_score = -1e30
clip_ratio = 0.05
adam_eps = 1e-08
decay_rate = 0.1
ALL = ("z", "x", "core", "y")
f32 = jnp.float32
bf16 = jnp.bfloat16
LANES = 128
TILE = 256
VMEM_BYTES = 56 * 2**20

TAIL_SLOPE = 0.275
TAIL_POLY = (
    0.10971068582446765,
    0.1096543595961662,
    0.10219045697718625,
    0.07893593678575173,
    0.08800740710695068,
    -0.03516190352887128,
    0.13017028940734943,
    -0.11067510560848658,
    0.027167870070925505,
)


def mm(a, b):
    return jnp.dot(a, b, preferred_element_type=f32)


def mm_t(a, b):
    return lax.dot_general(a, b, (((1,), (1,)), ((), ())), preferred_element_type=f32)


def gelu_parts(v):
    a = jnp.abs(v)
    bell = jnp.exp(v * v * -0.5)
    t = 1.0 / (1.0 + TAIL_SLOPE * a)
    poly = jnp.full_like(v, TAIL_POLY[-1])
    for factor in TAIL_POLY[-2::-1]:
        poly = poly * t + factor
    tail = poly * t * bell
    return jnp.where(v >= 0.0, 1.0 - tail, tail), bell * (1.0 / math.sqrt(2.0 * math.pi))


def norm_stats(values):
    center = values - jnp.mean(values, axis=-1, keepdims=True)
    rstd = lax.rsqrt(jnp.mean(center * center, axis=-1, keepdims=True) + ln_eps)
    return center * rstd, rstd


def norm_back(grad, values, gain_row):
    unit, rstd = norm_stats(values)
    grad = grad * gain_row
    mean_grad = jnp.mean(grad, axis=-1, keepdims=True)
    mean_dot = jnp.mean(grad * unit, axis=-1, keepdims=True)
    return rstd * (grad - mean_grad - unit * mean_dot)


def places():
    _, x, core, y = (lax.axis_index(axis) for axis in ALL)
    found = []
    for other in range(2):
        c = lax.rem(core + other, 2)
        for dx, dy in ((0, 0), (1 - c, c), (c, 1 - c), (1, 1)):
            found.append((lax.rem(x + dx, 2), c, lax.rem(y + dy, 2)))
    return found


def ring_place(back, size):
    return lax.rem(lax.axis_index("z") + size - back, size)


class Copies:
    def __init__(self, pairs, sems):
        self.copies = [
            pltpu.make_async_copy(source, target, sems.at[i])
            for i, (source, target) in enumerate(pairs)
        ]

    def start(self):
        for copy in self.copies:
            copy.start()
        return self

    def wait(self):
        for copy in self.copies:
            copy.wait()


def weight_copies(refs, column, width, dest, sems, ringed):
    if len(refs) == 1:
        return Copies([(refs[0].at[:, pl.ds(column, dest.shape[-1])], dest)], sems)
    z_size, rows, _ = refs[0].shape
    columns = pl.ds(column, width)
    pairs = []
    for ref, (x, core, y) in zip(refs, places()):
        to_rows = pl.ds(pl.multiple_of((x * 2 + core) * rows, 16), rows)
        to_columns = pl.ds(pl.multiple_of(y * width, LANES), width)
        if ringed:
            for back in range(z_size):
                at = ring_place(back, z_size)
                pairs.append((ref.at[back, :, columns], dest.at[at, to_rows, to_columns]))
        else:
            pairs.append((ref.at[:, :, columns], dest.at[:, to_rows, to_columns]))
    return Copies(pairs, sems)


def rider_copies(refs, column, dest, sems):
    z_size = refs[0].shape[0]
    pairs = []
    for ref, (x, core, y) in zip(refs, places()):
        for back in range(z_size):
            at = ((ring_place(back, z_size) * 2 + x) * 2 + core) * 2 + y
            pairs.append((ref.at[back, :, pl.ds(column, LANES)], dest.at[at]))
    return Copies(pairs, sems)


def rows_view(ref, columns=None):
    value = ref[...] if columns is None else ref[..., columns]
    return value.reshape(-1, value.shape[-1])


def weight_scratch(refs, width, columns):
    if len(refs) == 1:
        return pltpu.VMEM((width, columns), bf16)
    z_size, rows, _ = refs[0].shape
    return pltpu.VMEM((z_size, width // z_size, columns), bf16)


def column_tile(at):
    return pl.ds(pl.multiple_of(at * TILE, TILE), TILE)


def pair_lanes(at):
    return pl.ds(pl.multiple_of(at * LANES, LANES), LANES)


def head_of(pair, head):
    lane = lax.broadcasted_iota(jnp.int32, pair.shape, 1)
    keep = (lane < HEAD_DIM) if head == 0 else (lane >= HEAD_DIM)
    return jnp.where(keep, pair, jnp.zeros_like(pair))


def fill_bias(bias_ref, seg_col_ref, seg_row_ref):
    bias_ref[...] = jnp.where(seg_col_ref[...] == seg_row_ref[...], 0.0, masked_score)


def attn_forward_body(static, *refs):
    count, ringed, layer_at, slot_total, takes_riders = static
    pieces, refs = refs[:count], refs[count:]
    x_ref, slot_ref, base_ref, seg_col_ref, seg_row_ref, gain_ref = refs[:6]
    refs = refs[6:]
    rider_ref = refs[4] if takes_riders else refs[0]
    entry_ref, qkv_ref, lse_ref, middle_ref = refs[:4] if takes_riders else refs[1:5]
    w_qkv, w_out, norm_ref, mixed_ref, bias_ref, sem_a, sem_b, sem_c = refs[5:]
    tokens, width = entry_ref.shape
    y_size = 1 if count == 1 else 2
    cut = 3 * width // y_size
    if takes_riders:
        load_riders = rider_copies(pieces, cut + width // y_size, rider_ref, sem_c).start()
    load_qkv = weight_copies(pieces, 0, cut, w_qkv, sem_a, ringed).start()
    load_out = weight_copies(pieces, cut, width // y_size, w_out, sem_b, ringed).start()
    fill_bias(bias_ref, seg_col_ref, seg_row_ref)
    slots = slot_ref[...]
    onehot = (slots == base_ref[...]).astype(bf16)
    is_prompt = slots < slot_total
    if takes_riders:
        load_riders.wait()
    holders = base_ref.shape[1] // 8
    windows = rider_ref[layer_at * holders : (layer_at + 1) * holders].astype(f32)
    for at in range(width // LANES):
        lanes = slice(at * LANES, (at + 1) * LANES)
        part = windows[:, at * 8 : (at + 1) * 8, :].reshape(-1, LANES)
        inject = mm(onehot, part.astype(bf16))
        entry_ref[:, lanes] = jnp.where(is_prompt, inject, x_ref[:, lanes].astype(f32))
    norm_ref[...] = (norm_stats(entry_ref[...])[0] * gain_ref[...]).astype(bf16)
    load_qkv.wait()

    @pl.loop(0, 3 * width // TILE)
    def _(at):
        columns = column_tile(at)
        scale = jnp.where(at < width // TILE, HEAD_DIM**-0.5, 1.0)
        out = mm(norm_ref[...], rows_view(w_qkv, columns)).astype(bf16)
        qkv_ref[:, columns] = (out.astype(f32) * scale).astype(bf16)

    pairs = width // LANES

    @pl.loop(0, pairs)
    def _(at):
        query, key = qkv_ref[:, pair_lanes(at)], qkv_ref[:, pair_lanes(at + pairs)]
        value_t = qkv_ref[:, pair_lanes(at + 2 * pairs)].T
        mixed = []
        for head in range(2):
            query_head = head_of(query, head)
            tiles, lses = [], []
            for t in range(tokens // TILE):
                q_rows = slice(t * TILE, (t + 1) * TILE)
                scores = mm_t(key, query_head[q_rows]) + bias_ref[:, q_rows]
                top = jnp.max(scores, axis=0, keepdims=True)
                exponent = jnp.exp(scores - top)
                total = jnp.sum(exponent, axis=0, keepdims=True)
                part = mm(value_t[head * HEAD_DIM : (head + 1) * HEAD_DIM], exponent.astype(bf16))
                tiles.append((part * (1.0 / total)).astype(bf16))
                lses.append(top + jnp.log(total))
            mixed.append(jnp.concatenate(tiles, axis=1))
            lse_ref[pl.ds(2 * at + head, 1), :] = jnp.concatenate(lses, axis=1)
        mixed_ref[:, pair_lanes(at)] = jnp.concatenate(mixed, axis=0).T

    load_out.wait()

    @pl.loop(0, width // TILE)
    def _(at):
        columns = column_tile(at)
        middle_ref[:, columns] = entry_ref[:, columns] + mm(
            mixed_ref[...], rows_view(w_out, columns)
        )


def attn_backward_body(static, *refs):
    count, ringed = static
    pieces, refs = refs[:count], refs[count:]
    grad_ref, entry_ref, qkv_ref, lse_ref = refs[:4]
    slot_col_ref, slot_row_ref, seg_col_ref, seg_row_ref, gain_ref = refs[4:9]
    out_ref, prompt_ref = refs[9:11]
    w_qkv, w_out, low_ref, mixed_ref, dqkv_ref, bias_ref, sem_a, sem_b = refs[11:]
    tokens, width = entry_ref.shape
    y_size = 1 if count == 1 else 2
    cut = 3 * width // y_size
    load_out = weight_copies(pieces, cut, width // y_size, w_out, sem_b, ringed).start()
    load_qkv = weight_copies(pieces, 0, cut, w_qkv, sem_a, ringed).start()
    low_ref[...] = grad_ref[...].astype(bf16)
    fill_bias(bias_ref, seg_col_ref, seg_row_ref)
    load_out.wait()
    mixed_ref[...] = mm_t(low_ref[...], rows_view(w_out)).astype(bf16)
    pairs = width // LANES

    @pl.loop(0, pairs)
    def _(at):
        query, key = qkv_ref[:, pair_lanes(at)], qkv_ref[:, pair_lanes(at + pairs)]
        value, grad = qkv_ref[:, pair_lanes(at + 2 * pairs)], mixed_ref[:, pair_lanes(at)]
        key_t = key.T
        d_key = jnp.zeros((tokens, LANES), f32)
        d_value = jnp.zeros((tokens, LANES), f32)
        d_query_t = []
        for head in range(2):
            query_head, grad_head = head_of(query, head), head_of(grad, head)
            lse = lse_ref[pl.ds(2 * at + head, 1), :]
            tiles = []
            for t in range(tokens // TILE):
                q_rows = slice(t * TILE, (t + 1) * TILE)
                scores = mm_t(key, query_head[q_rows]) + bias_ref[:, q_rows]
                probs = jnp.exp(scores - lse[:, q_rows])
                grad_probs = mm_t(value, grad_head[q_rows])
                inner = jnp.sum(probs * grad_probs, axis=0, keepdims=True)
                d_scores = (probs * (grad_probs - inner)).astype(bf16)
                d_value = d_value + mm(probs.astype(bf16), grad_head[q_rows])
                d_key = d_key + mm(d_scores, query_head[q_rows])
                tiles.append(mm(key_t[head * HEAD_DIM : (head + 1) * HEAD_DIM], d_scores))
            d_query_t.append(jnp.concatenate(tiles, axis=1))
        d_query = jnp.concatenate(d_query_t, axis=0) * HEAD_DIM**-0.5
        dqkv_ref[:, pair_lanes(at)] = d_query.astype(bf16).T
        dqkv_ref[:, pair_lanes(at + pairs)] = d_key.astype(bf16)
        dqkv_ref[:, pair_lanes(at + 2 * pairs)] = d_value.astype(bf16)

    load_qkv.wait()
    grad_norm = mm_t(dqkv_ref[...], rows_view(w_qkv))
    grad_entry = grad_ref[...] + norm_back(grad_norm, entry_ref[...], gain_ref[...])
    slot_total = prompt_ref.shape[0]
    onehot_t = (
        slot_row_ref[...] == lax.broadcasted_iota(jnp.int32, (slot_total, tokens), 0)
    ).astype(bf16)
    high = grad_entry.astype(bf16)
    low = (grad_entry - high.astype(f32)).astype(bf16)
    prompt_ref[...] = mm(onehot_t, high) + mm(onehot_t, low)
    out_ref[...] = jnp.where(slot_col_ref[...] < slot_total, 0.0, grad_entry)


def mlp_forward_body(static, *refs):
    count, ringed = static
    pieces, refs = refs[:count], refs[count:]
    middle_ref, gain_ref = refs[:2]
    hidden_ref, slope_ref = refs[2:4]
    w_up, w_down, norm_ref, active_ref, sem_a, sem_b = refs[4:]
    units = slope_ref.shape[1]
    width = middle_ref.shape[1]
    cut = units // (1 if count == 1 else 2)
    load_up = weight_copies(pieces, 0, cut, w_up, sem_a, ringed).start()
    load_down = weight_copies(pieces, cut, cut, w_down, sem_b, ringed).start()
    norm_ref[...] = (norm_stats(middle_ref[...])[0] * gain_ref[...]).astype(bf16)
    load_up.wait()

    @pl.loop(0, units // TILE)
    def _(at):
        columns = column_tile(at)
        before = mm(norm_ref[...], rows_view(w_up, columns))
        phi_sum, phi = gelu_parts(before)
        active_ref[:, columns] = (before * phi_sum).astype(bf16)
        slope_ref[:, columns] = (phi_sum + before * phi).astype(bf16)

    load_down.wait()
    branch = mm_t(active_ref[...], rows_view(w_down))
    hidden_ref[...] = (middle_ref[...] + branch).astype(hidden_ref.dtype)


def mlp_backward_body(static, *refs):
    count, ringed = static
    pieces, refs = refs[:count], refs[count:]
    grad_ref, middle_ref, slope_ref, gain_ref = refs[:4]
    (out_ref,) = refs[4:5]
    w_up, w_down, low_ref, before_ref, sem_a, sem_b = refs[5:]
    units = slope_ref.shape[1]
    width = middle_ref.shape[1]
    cut = units // (1 if count == 1 else 2)
    load_down = weight_copies(pieces, cut, cut, w_down, sem_b, ringed).start()
    load_up = weight_copies(pieces, 0, cut, w_up, sem_a, ringed).start()
    low_ref[...] = grad_ref[...].astype(bf16)
    load_down.wait()

    @pl.loop(0, units // TILE)
    def _(at):
        columns = column_tile(at)
        grad_active = mm(low_ref[...], rows_view(w_down, columns))
        before_ref[:, columns] = (grad_active * slope_ref[:, columns].astype(f32)).astype(bf16)

    load_up.wait()
    grad_norm = mm_t(before_ref[...], rows_view(w_up))
    back = norm_back(grad_norm, middle_ref[...], gain_ref[...])
    out_ref[...] = grad_ref[...].astype(f32) + back


def shape(dims, dtype):
    return jax.ShapeDtypeStruct(dims, dtype)


def run(body, static, pieces, inputs, outputs, scratch, flops, name):
    whole = pl.BlockSpec(memory_space=pltpu.VMEM)
    away = pl.BlockSpec(memory_space=pl.ANY)
    moved = sum(math.prod(a.shape) * a.dtype.itemsize for a in (*pieces, *inputs, *outputs))
    return pl.pallas_call(
        partial(body, (len(pieces), *static)),
        out_shape=outputs,
        in_specs=[away] * len(pieces) + [whole] * len(inputs),
        out_specs=[whole] * len(outputs),
        scratch_shapes=scratch,
        compiler_params=pltpu.CompilerParams(vmem_limit_bytes=VMEM_BYTES),
        cost_estimate=pl.CostEstimate(flops=flops, transcendentals=0, bytes_accessed=moved),
        name=name,
    )(*pieces, *inputs)


def piece_sems(pieces, ringed):
    count = len(pieces) * (pieces[0].shape[0] if ringed and len(pieces) > 1 else 1)
    return pltpu.SemaphoreType.DMA((count,))


def attn_forward(pieces, ringed, layer_at, slot_total, x, riders, marks, gain):
    tokens, width = x.shape
    pairs = width // LANES
    devices = math.prod(axis_sizes())
    takes_riders = riders is None
    outputs = (
        shape((tokens, width), f32),
        shape((tokens, 3 * width), bf16),
        shape((2 * pairs, tokens), f32),
        shape((tokens, width), f32),
    )
    inputs = (x, marks["slot_col"], marks["base"], marks["seg_col"], marks["seg_row"], gain)
    if takes_riders:
        outputs += (shape((devices, 8 * pairs, LANES), bf16),)
    else:
        inputs += (riders,)
    scratch = [
        weight_scratch(pieces, width, 3 * width),
        weight_scratch(pieces, width, width),
        pltpu.VMEM((tokens, width), bf16),
        pltpu.VMEM((tokens, width), bf16),
        pltpu.VMEM((tokens, tokens), f32),
        piece_sems(pieces, ringed),
        piece_sems(pieces, ringed),
        piece_sems(pieces, ringed),
    ]
    flops = 2 * tokens * width * (4 * width + 2 * tokens)
    static = (ringed, layer_at, slot_total, takes_riders)
    found = run(
        attn_forward_body, static, pieces, inputs, outputs, scratch, flops, "attn_forward"
    )
    return found if takes_riders else (*found, riders)


def attn_backward(pieces, ringed, grad, entry, qkv, lse, marks, gain, slot_total):
    tokens, width = entry.shape
    outputs = (shape((tokens, width), f32), shape((slot_total, width), f32))
    scratch = [
        weight_scratch(pieces, width, 3 * width),
        weight_scratch(pieces, width, width),
        pltpu.VMEM((tokens, width), bf16),
        pltpu.VMEM((tokens, width), bf16),
        pltpu.VMEM((tokens, 3 * width), bf16),
        pltpu.VMEM((tokens, tokens), f32),
        piece_sems(pieces, ringed),
        piece_sems(pieces, ringed),
    ]
    flops = 2 * tokens * width * (4 * width + 5 * tokens)
    inputs = (
        grad,
        entry,
        qkv,
        lse,
        marks["slot_col"],
        marks["slot_row"],
        marks["seg_col"],
        marks["seg_row"],
        gain,
    )
    return run(
        attn_backward_body, (ringed,), pieces, inputs, outputs, scratch, flops, "attn_backward"
    )


def mlp_forward(pieces, ringed, middle, gain, units, dtype):
    tokens, width = middle.shape
    outputs = (shape((tokens, width), dtype), shape((tokens, units), bf16))
    scratch = [
        weight_scratch(pieces, width, units),
        weight_scratch(pieces, width, units),
        pltpu.VMEM((tokens, width), bf16),
        pltpu.VMEM((tokens, units), bf16),
        piece_sems(pieces, ringed),
        piece_sems(pieces, ringed),
    ]
    flops = 4 * tokens * width * units
    return run(
        mlp_forward_body, (ringed,), pieces, (middle, gain), outputs, scratch, flops, "mlp_forward"
    )


def mlp_backward(pieces, ringed, grad, middle, slope, gain):
    tokens, width = middle.shape
    units = slope.shape[1]
    scratch = [
        weight_scratch(pieces, width, units),
        weight_scratch(pieces, width, units),
        pltpu.VMEM((tokens, width), bf16),
        pltpu.VMEM((tokens, units), bf16),
        piece_sems(pieces, ringed),
        piece_sems(pieces, ringed),
    ]
    flops = 4 * tokens * width * units
    inputs = (grad, middle, slope, gain)
    outputs = (shape((tokens, width), f32),)
    return run(
        mlp_backward_body, (ringed,), pieces, inputs, outputs, scratch, flops, "mlp_backward"
    )[0]


def axis_sizes():
    return tuple(lax.axis_size(axis) for axis in ALL)


def is_block():
    return axis_sizes() == (4, 2, 2, 2)


def flip(value, axis):
    return lax.ppermute(value, axis, [(0, 1), (1, 0)])


def turn(value, core_of_x):
    moves = []
    z_size, x_size, core_size, y_size = axis_sizes()
    for z in range(z_size):
        for x in range(x_size):
            for core in range(core_size):
                for y in range(y_size):
                    at = ((z * x_size + x) * core_size + core) * y_size + y
                    along_x = core == core_of_x
                    to_x, to_y = (1 - x, y) if along_x else (x, 1 - y)
                    moves.append((at, ((z * x_size + to_x) * core_size + core) * y_size + to_y))
    return lax.ppermute(value, ALL, moves)


def ring_z(value):
    size = lax.axis_size("z")
    parts = [value]
    for step in range(1, size):
        parts.append(lax.ppermute(value, "z", [(i, (i + step) % size) for i in range(size)]))
    return jnp.stack(parts)


def to_all(along_z):
    first = turn(along_z, 0)
    second = turn(along_z, 1)
    third = turn(first, 1)
    own = [along_z, first, second, third]
    return own + [flip(piece, "core") for piece in own]


def total_over(value):
    if not is_block():
        return lax.psum(value, ALL)
    core = lax.axis_index("core")
    low = value.astype(bf16)
    mine = jnp.where(core == 0, value[0], value[1])
    theirs = jnp.where(core == 0, low[1], low[0])
    total = mine + flip(theirs, "core").astype(f32)
    for axis in ("x", "y"):
        total = total + flip(total.astype(bf16), axis).astype(f32)
    for pairs in ([(0, 1), (1, 0), (2, 3), (3, 2)], [(0, 2), (2, 0), (1, 3), (3, 1)]):
        total = total + lax.ppermute(total.astype(bf16), "z", pairs).astype(f32)
    other = flip(total.astype(bf16), "core").astype(f32)
    return jnp.stack([jnp.where(core == 0, total, other), jnp.where(core == 0, other, total)])


def halves(values):
    high = values.astype(bf16)
    return high, (values - high.astype(f32)).astype(bf16)


def window_rows(count, width):
    step = math.gcd(count, width)
    return -(-(width - step + count) // width)


def prompt_window(prompts, width):
    count = prompts.shape[0]
    assert window_rows(count, width) <= 4
    shift = lax.axis_index(ALL) * count % width
    flat = lax.dynamic_update_slice(jnp.zeros((4 * width,), f32), prompts, (shift,))
    rows = flat.reshape(4, width // LANES, LANES).transpose(1, 0, 2)
    return jnp.concatenate(halves(rows), axis=1).reshape(-1, LANES)


def window_slots(count, width, layers):
    holders = math.prod(axis_sizes()) // layers
    base = jnp.arange(holders, dtype=jnp.int32) * count // width
    both = base[:, None] + jnp.arange(8, dtype=jnp.int32)[None, :] % 4
    return both.reshape(1, -1)


def gather_block(attn_parts, mlp_parts, window, layers):
    attn_width = attn_parts[0].shape[1]
    start = jnp.concatenate([attn_parts[0], window], axis=1)
    pieces = [to_all(ring_z(start)), to_all(lax.all_gather(mlp_parts[0], "z"))]
    for layer_at in range(1, layers):
        both = jnp.concatenate([attn_parts[layer_at], mlp_parts[layer_at]], axis=1)
        along = lax.all_gather(both, "z")
        pieces.append(to_all(along[..., :attn_width]))
        pieces.append(to_all(along[..., attn_width:]))
    return pieces, [True] + [False] * (2 * layers - 1)


def gather_any(qkv, out, up, down):
    seq = ("z", "x", "core")
    pieces = []
    for layer_at in range(qkv.shape[0]):
        attn = jnp.concatenate([qkv[layer_at], out[layer_at]], axis=1)
        pieces.append([lax.all_gather(attn, seq, tiled=True)])
        mlp = []
        for part in (up[layer_at], down[layer_at].T):
            part = lax.all_gather(part, "y", axis=1, tiled=True)
            mlp.append(lax.all_gather(part, seq, tiled=True))
        pieces.append([jnp.concatenate(mlp, axis=1)])
    return pieces, [False] * len(pieces)


def per_device(
    patches,
    segments,
    prompt_slots,
    norm_gains,
    qkv_weight,
    out_weight,
    up_weight,
    down_weight,
    cotangent,
    prompts,
    first_moment,
    second_moment,
    adam_betas,
    learn_rate,
):
    layers, _, width = norm_gains.shape
    tokens = patches.shape[0]
    units = up_weight.shape[2] * lax.axis_size("y")
    total_prompts = prompts.shape[0] * math.prod(axis_sizes())
    slot_total = total_prompts // (layers * width)
    window = prompt_window(prompts, width)
    if is_block():
        y_size, y_at = lax.axis_size("y"), lax.axis_index("y")
        rows = qkv_weight.shape[1]
        cut, out_cut = qkv_weight.shape[2] // y_size, width // y_size
        attn_parts, mlp_parts = [], []
        for layer_at in range(layers):
            qkv = lax.dynamic_slice(qkv_weight[layer_at], (0, y_at * cut), (rows, cut))
            out = lax.dynamic_slice(out_weight[layer_at], (0, y_at * out_cut), (rows, out_cut))
            attn_parts.append(jnp.concatenate([qkv, out], axis=1))
            mlp_parts.append(
                jnp.concatenate([up_weight[layer_at], down_weight[layer_at].T], axis=1)
            )
        pieces, ringed = gather_block(attn_parts, mlp_parts, window, layers)
        riders = None
    else:
        pieces, ringed = gather_any(qkv_weight, out_weight, up_weight, down_weight)
        riders = lax.all_gather(window, ALL)

    marks = {
        "base": window_slots(prompts.shape[0], width, layers),
        "slot_col": prompt_slots.reshape(tokens, 1),
        "slot_row": prompt_slots.reshape(1, tokens),
        "seg_col": segments.reshape(tokens, 1),
        "seg_row": segments.reshape(1, tokens),
    }
    gains = norm_gains.reshape(2 * layers, 1, width)
    hidden = patches
    kept = []
    for layer_at in range(layers):
        attn, mlp = 2 * layer_at, 2 * layer_at + 1
        entry, qkv, lse, middle, riders = attn_forward(
            pieces[attn],
            ringed[attn],
            layer_at,
            slot_total,
            hidden,
            riders,
            marks,
            gains[attn],
        )
        dtype = bf16 if layer_at == layers - 1 else f32
        hidden, slope = mlp_forward(pieces[mlp], ringed[mlp], middle, gains[mlp], units, dtype)
        kept.append((entry, qkv, lse, middle, slope))
    block_output = hidden
    gradient = cotangent
    layer_grads = []
    for layer_at in reversed(range(layers)):
        attn, mlp = 2 * layer_at, 2 * layer_at + 1
        entry, qkv, lse, middle, slope = kept[layer_at]
        gradient = mlp_backward(pieces[mlp], ringed[mlp], gradient, middle, slope, gains[mlp])
        gradient, layer_grad = attn_backward(
            pieces[attn], ringed[attn], gradient, entry, qkv, lse, marks, gains[attn], slot_total
        )
        layer_grads.append(layer_grad)

    prompt_grad = total_over(jnp.stack(layer_grads[::-1]))
    grad_norm = jnp.sqrt(jnp.sum(prompt_grad * prompt_grad))
    clip_limit = clip_ratio * math.sqrt(total_prompts)
    own_grads = lax.dynamic_slice(
        prompt_grad.reshape(-1), (lax.axis_index(ALL) * prompts.shape[0],), prompts.shape
    )
    clipped = own_grads * jnp.minimum(1.0, clip_limit / (grad_norm + 1e-06))
    beta_one = adam_betas[0]
    beta_two = adam_betas[1]
    step_value = float(ADAM_STEP)
    new_first = beta_one * first_moment + (1.0 - beta_one) * clipped
    new_second = beta_two * second_moment + (1.0 - beta_two) * clipped * clipped
    first_hat = new_first / (1.0 - beta_one**step_value)
    second_hat = new_second / (1.0 - beta_two**step_value)
    new_prompts = prompts - learn_rate[0] * (
        first_hat / (jnp.sqrt(second_hat) + adam_eps) + decay_rate * prompts
    )
    return (block_output, gradient, new_prompts, new_first, new_second, grad_norm.reshape(1))


def solution(mesh):
    seq_size, mlp_size = mesh.shape["seq"], mesh.shape["mlp"]
    grid = Mesh(mesh.devices.reshape(seq_size // 4, 2, 2, mlp_size), ALL)
    seq, mlp = ("z", "x", "core"), "y"
    in_specs = (
        P(ALL, None),
        P(ALL),
        P(ALL),
        P(),
        P(None, seq, None),
        P(None, seq, None),
        P(None, seq, mlp),
        P(None, mlp, seq),
        P(ALL, None),
        P(ALL),
        P(ALL),
        P(ALL),
        P(),
        P(),
    )
    out_specs = (P(ALL, None), P(ALL, None), P(ALL), P(ALL), P(ALL), P())
    return jax.shard_map(
        per_device, mesh=grid, in_specs=in_specs, out_specs=out_specs, check_vma=False
    )
```

time: 522 us -> 372 us (0.71); the launches traced: 513 us -> 372 us
  matrix products: 156 us -> 0 us
  Pallas kernels: 0 us -> 155 us
  local copies, waits for them, and re-layouts: 129 us -> 12.3 us
  other arithmetic: 89.7 us -> 5.54 us
  waiting for transfers between devices: 35.2 us -> 110 us
  blocking collectives: 43.2 us -> 0 us
  starting transfers between devices: 37 us -> 67.6 us
    dot_general x30 -> x0, matrix products: 156 us -> none  [the longest x2 36.8 us: per_device(): before = jnp.dot(normed_two.astype(bf16), w_up, preferred_element_type=f32)]
    pallas_call x0 -> x8, Pallas kernels: none -> 155 us  [run(): pl.pallas_call(partial(body, (len(pieces), *static)), out_shape=outputs,...]
    ppermute x0 -> x12, waiting for transfers between devices: none -> 62.5 us  [turn(): return lax.ppermute(value, ALL, moves)]
    all_gather x1 -> x0, blocking collectives: 43.2 us -> none  [gather_group(): along = ring_z(both) if first else lax.all_gather(both, 'z')]
    transpose x8 -> x0, local copies, waits for them, and re-layouts: 38.3 us -> none  [the longest x7 38.2 us: gather_group(): return (a.transpose(3, 2, 0, 4, 1, 5), b.transpose(3, 1, 0, 4, 2, 5))]
    unnamed x232 -> x50, local copies, waits for them, and re-layouts: 41.5 us -> 3.82 us
    another operation x37 -> x2, other arithmetic: 36.4 us -> 0.12 us  [ring_z(): return jnp.stack(parts)]
    ppermute x28 -> x20, waiting for transfers between devices: 35.2 us -> 5.52 us  [flip(): return lax.ppermute(value, axis, [(0, 1), (1, 0)])]
  transfers between devices with their start and end apart: 35 -> 39, of which waited for: 11 -> 14; matrix products, arithmetic and copies ran while one was open for 31% -> 2% of each run, Pallas kernels for 0% -> 17%
where the time goes in v2:
time: 372 us
  Pallas kernels  155 us (42%)
  waiting for transfers between devices  110 us (30%)
  starting transfers between devices  67.6 us (18%)
  between operations  20.7 us (6%)
  local copies, waits for them, and re-layouts  12.3 us (3%)
  other arithmetic  5.54 us (1%)
    pallas_call x8, Pallas kernels, run(): pl.pallas_call(partial(body, (len(pieces), *static)), out_shape=outputs,...  155 us
    ppermute x12, waiting for transfers between devices, turn(): return lax.ppermute(value, ALL, moves)  62.5 us
    ppermute x20, starting transfers between devices, flip(): return lax.ppermute(value, axis, [(0, 1), (1, 0)])  42.3 us
    all_gather x1, waiting for transfers between devices, gather_block(): along = lax.all_gather(both, 'z')  19.1 us
    ppermute x3, waiting for transfers between devices, ring_z(): lax.ppermute(value, 'z', [(i, (i + step) % size) for i in range(size)])  18.8 us
    ppermute x12, starting transfers between devices, turn(): return lax.ppermute(value, ALL, moves)  14.3 us
  transfers between devices with their start and end apart: 39, of which 14 were waited for; matrix products, arithmetic and copies ran while one was open for 2% of the time, Pallas kernels for 17%

profile of v2, /device:TPU:1, one launch (start us, length us, event | category | flops | bytes accessed | tf_op | source)
XLA Modules:
  0.0 371.9 jit_solution(912024818242804955)
XLA Ops:
  11.6 4.2 %collective-permute-start.23 = (bf16[48,1664]{1,0:T(8,128)(2,1)S(1)}, bf16[48,1664]{1,0:T(8,128)(2,1)S(1)}, u32[]{:S(2)}, u32[]{:S(2)}) collective-permute-start(bf16[48,1664]{1,0:T(8,128)(2,1)S(1)} %get-tuple-element.60), channel_id=1, source_target_pairs={{0,24},{8,0},{16,8},{24,16},{1,25},{9,1},{17,9},{25,17},{2,26},{10... | collective-permute-start | bytes 479240 | tf_op jit(solution)/shard_map/ppermute | solution.py:502
  16.2 2.4 collective-permute-done.23
  18.6 16.4 %collective-permute-done.22 = bf16[48,1664]{1,0:T(8,128)(2,1)S(1)} collective-permute-done((bf16[48,1664]{1,0:T(8,128)(2,1)S(1)}, bf16[48,1664]{1,0:T(8,128)(2,1)S(1)}, u32[]{:S(2)}, u32[]{:S(2)}) %collective-permute-start.22) | collective-permute-done | bytes 159776 | tf_op jit(solution)/shard_map/ppermute | solution.py:502
  37.7 4.3 %collective-permute-start.27 = (bf16[4,48,1664]{2,1,0:T(8,128)(2,1)S(1)}, bf16[4,48,1664]{2,1,0:T(8,128)(2,1)S(1)}, u32[]{:S(2)}, u32[]{:S(2)}) collective-permute-start(bf16[4,48,1664]{2,1,0:T(8,128)(2,1)S(1)} %pad_maximum_fusion.refs_0_), channel_id=1, source_target_pairs={{0,2},{2,0},{1,3},{3,1},{4,6},{6,4},{5,7},{7,5},{8,10},{10,8},{9,1... | collective-permute-start | bytes 1916936 | tf_op jit(solution)/shard_map/ppermute | solution.py:481
  42.0 4.0 %collective-permute-done.24.refs_1_ = bf16[4,48,1664]{2,1,0:T(8,128)(2,1)S(1)} collective-permute-done((bf16[4,48,1664]{2,1,0:T(8,128)(2,1)S(1)}, bf16[4,48,1664]{2,1,0:T(8,128)(2,1)S(1)}, u32[]{:S(2)}, u32[]{:S(2)}) %collective-permute-start.24) | collective-permute-done | bytes 639008 | tf_op jit(solution)/shard_map/ppermute | solution.py:495
  46.0 2.2 collective-permute-start.26
  48.2 8.1 %collective-permute-start.28 = (bf16[4,48,1664]{2,1,0:T(8,128)(2,1)S(1)}, bf16[4,48,1664]{2,1,0:T(8,128)(2,1)}, u32[]{:S(2)}, u32[]{:S(2)}) collective-permute-start(bf16[4,48,1664]{2,1,0:T(8,128)(2,1)S(1)} %collective-permute-done.24.refs_1_), channel_id=1, source_target_pairs={{0,2},{2,0},{1,3},{3,1},{4,6},{6,4},{5,7},{7,5},{8,10},{10,8},{9,1... | collective-permute-start | bytes 1916936 | tf_op jit(solution)/shard_map/ppermute | solution.py:481
  56.3 1.7 collective-permute-start.14
  59.8 13.8 %collective-permute-start.29 = (bf16[4,48,1664]{2,1,0:T(8,128)(2,1)S(1)}, bf16[4,48,1664]{2,1,0:T(8,128)(2,1)}, u32[]{:S(2)}, u32[]{:S(2)}) collective-permute-start(bf16[4,48,1664]{2,1,0:T(8,128)(2,1)S(1)} %collective-permute-done.25.refs_2_), channel_id=1, source_target_pairs={{0,2},{2,0},{1,3},{3,1},{4,6},{6,4},{5,7},{7,5},{8,10},{10,8},{9,1... | collective-permute-start | bytes 1916936 | tf_op jit(solution)/shard_map/ppermute | solution.py:481
  73.6 19.1 %all-gather.5.cloned.1.call-done = bf16[192,4608]{1,0:T(8,128)(2,1)} async-done(((bf16[48,4608]{1,0:T(8,128)(2,1)}), bf16[192,4608]{1,0:T(8,128)(2,1)}) %all-gather.5.cloned.1.call-update) | async-done | bytes 1769488 | tf_op jit(solution)/shard_map/all_gather | solution.py:562
  95.2 1.3 slice.70.refs_0_
  99.6 5.1 %collective-permute-done.7.refs_1_ = bf16[4,48,1536]{2,1,0:T(8,128)(2,1)S(1)} collective-permute-done((bf16[4,48,1536]{2,1,0:T(8,128)(2,1)S(1)}, bf16[4,48,1536]{2,1,0:T(8,128)(2,1)S(1)}, u32[]{:S(2)}, u32[]{:S(2)}) %collective-permute-start.7) | collective-permute-done | bytes 589856 | tf_op jit(solution)/shard_map/ppermute | solution.py:495
  104.7 4.4 %collective-permute-start.10 = (bf16[4,48,1536]{2,1,0:T(8,128)(2,1)S(1)}, bf16[4,48,1536]{2,1,0:T(8,128)(2,1)S(1)}, u32[]{:S(2)}, u32[]{:S(2)}) collective-permute-start(bf16[4,48,1536]{2,1,0:T(8,128)(2,1)S(1)} %slice.71.refs_0_), channel_id=1, source_target_pairs={{0,2},{2,0},{1,3},{3,1},{4,6},{6,4},{5,7},{7,5},{8,10},{10,8},{9,1... | collective-permute-start | bytes 1769480 | tf_op jit(solution)/shard_map/ppermute | solution.py:481
  109.0 26.8 %collective-permute-done.8.refs_2_ = bf16[4,48,1536]{2,1,0:T(8,128)(2,1)} collective-permute-done((bf16[4,48,1536]{2,1,0:T(8,128)(2,1)S(1)}, bf16[4,48,1536]{2,1,0:T(8,128)(2,1)}, u32[]{:S(2)}, u32[]{:S(2)}) %collective-permute-start.8) | collective-permute-done | bytes 589856 | tf_op jit(solution)/shard_map/ppermute | solution.py:495
  137.7 16.8 %collective-permute-done.9.refs_3_ = bf16[4,48,1536]{2,1,0:T(8,128)(2,1)} collective-permute-done((bf16[4,48,1536]{2,1,0:T(8,128)(2,1)S(1)}, bf16[4,48,1536]{2,1,0:T(8,128)(2,1)}, u32[]{:S(2)}, u32[]{:S(2)}) %collective-permute-start.9) | collective-permute-done | bytes 589856 | tf_op jit(solution)/shard_map/ppermute | solution.py:495
  160.4 9.8 %collective-permute-done.2.refs_3_ = bf16[4,48,3072]{2,1,0:T(8,128)(2,1)} collective-permute-done((bf16[4,48,3072]{2,1,0:T(8,128)(2,1)}, bf16[4,48,3072]{2,1,0:T(8,128)(2,1)}, u32[]{:S(2)}, u32[]{:S(2)}) %collective-permute-start.2) | collective-permute-done | bytes 1179680 | tf_op jit(solution)/shard_map/ppermute | solution.py:495
  171.3 23.5 %attn_forward.2 = (f32[512,768]{1,0:T(8,128)}, bf16[512,2304]{1,0:T(8,128)(2,1)}, f32[12,512]{1,0:T(8,128)}, f32[512,768]{1,0:T(8,128)}, bf16[32,48,128]{2,1,0:T(8,128)(2,1)}) custom-call(bf16[4,48,1664]{2,1,0:T(8,128)(2,1)} %copy-done.2, bf16[4,48,1664]{2,1,0:T(8,128)(2,1)} %copy-done.18, bf16[4,48,1664]{2,1,0:T(8,128)(2,1)} %copy-done.19, ...), custom_call_target="tpu_custom_call" | custom-call | flops 3221225472 | bytes 11830784 | tf_op jit(solution)/shard_map/attn_forward/pallas_call | solution.py:355
  194.9 17.9 %mlp_forward.2 = (f32[512,768]{1,0:T(8,128)}, bf16[512,3072]{1,0:T(8,128)(2,1)}) custom-call(bf16[4,48,3072]{2,1,0:T(8,128)(2,1)} %bitcast.74, bf16[4,48,3072]{2,1,0:T(8,128)(2,1)} %collective-permute-done.14.refs_1_, bf16[4,48,3072]{2,1,0:T(8,128)(2,1)} %collective-permute-done.15.refs_2_, bf16[4,48,3072]{2,1,0:T(8,128)(2,1)} %collective-permute-done.16.refs_3_, ...), custom_call_target="tpu_custom_call" | custom-call | flops 4831838208 | bytes 15731712 | tf_op jit(solution)/shard_map/mlp_forward/pallas_call | solution.py:355
  213.6 21.6 %attn_forward.3 = (f32[512,768]{1,0:T(8,128)}, bf16[512,2304]{1,0:T(8,128)(2,1)}, f32[12,512]{1,0:T(8,128)}, f32[512,768]{1,0:T(8,128)}) custom-call(bf16[4,48,1536]{2,1,0:T(8,128)(2,1)} %copy-done.3, bf16[4,48,1536]{2,1,0:T(8,128)(2,1)} %copy-done.21, bf16[4,48,1536]{2,1,0:T(8,128)(2,1)} %collective-permute-done.8.refs_2_, ...), custom_call_target="tpu_custom_call" | custom-call | flops 3221225472 | bytes 12224000 | tf_op jit(solution)/shard_map/attn_forward/pallas_call | solution.py:355
  237.5 17.6 %mlp_forward.3 = (bf16[512,768]{1,0:T(8,128)(2,1)}, bf16[512,3072]{1,0:T(8,128)(2,1)}) custom-call(bf16[4,48,3072]{2,1,0:T(8,128)(2,1)} %copy-done, bf16[4,48,3072]{2,1,0:T(8,128)(2,1)} %collective-permute-done.refs_1_, bf16[4,48,3072]{2,1,0:T(8,128)(2,1)} %copy-done.13, bf16[4,48,3072]{2,1,0:T(8,128)(2,1)} %collective-permute-done.2.refs_3_, ...), custom_call_target="tpu_custom_call" | custom-call | flops 4831838208 | bytes 14945280 | tf_op jit(solution)/shard_map/mlp_forward/pallas_call | solution.py:355
  255.1 14.2 %mlp_backward.2.refs_8_ = f32[512,768]{1,0:T(8,128)} custom-call(bf16[4,48,3072]{2,1,0:T(8,128)(2,1)} %copy-done, bf16[4,48,3072]{2,1,0:T(8,128)(2,1)} %collective-permute-done.refs_1_, bf16[4,48,3072]{2,1,0:T(8,128)(2,1)} %copy-done.13, bf16[4,48,3072]{2,1,0:T(8,128)(2,1)} %collective-permute-done.2.refs_3_, bf16[4,48,3072]{2,1,0:T(8,128)(2,1)} %copy-done.14, ...), custom_call_target="tpu_custom_call" | custom-call | flops 4831838208 | bytes 16518144 | tf_op jit(solution)/shard_map/mlp_backward/pallas_call | solution.py:355
  269.3 22.3 %attn_backward.2 = (f32[512,768]{1,0:T(8,128)}, f32[50,768]{1,0:T(8,128)}) custom-call(bf16[4,48,1536]{2,1,0:T(8,128)(2,1)} %copy-done.3, bf16[4,48,1536]{2,1,0:T(8,128)(2,1)} %copy-done.21, bf16[4,48,1536]{2,1,0:T(8,128)(2,1)} %collective-permute-done.8.refs_2_, bf16[4,48,1536]{2,1,0:T(8,128)(2,1)} %collective-permute-done.9.refs_3_, ...), custom_call_target="tpu_custom_call" | custom-call | flops 4429185024 | bytes 11985920 | tf_op jit(solution)/shard_map/attn_backward/pallas_call | solution.py:355
  291.6 14.2 %mlp_backward.3.refs_8_ = f32[512,768]{1,0:T(8,128)} custom-call(bf16[4,48,3072]{2,1,0:T(8,128)(2,1)} %bitcast.75, bf16[4,48,3072]{2,1,0:T(8,128)(2,1)} %collective-permute-done.14.refs_1_, bf16[4,48,3072]{2,1,0:T(8,128)(2,1)} %collective-permute-done.15.refs_2_, bf16[4,48,3072]{2,1,0:T(8,128)(2,1)} %collective-permute-done.16.refs_3_, ...), custom_call_target="tpu_custom_call" | custom-call | flops 4831838208 | bytes 17304576 | tf_op jit(solution)/shard_map/mlp_backward/pallas_call | solution.py:355
  305.8 24.0 %attn_backward.3 = (f32[512,768]{1,0:T(8,128)}, f32[50,768]{1,0:T(8,128)}) custom-call(bf16[4,48,1664]{2,1,0:T(8,128)(2,1)} %copy-done.2, bf16[4,48,1664]{2,1,0:T(8,128)(2,1)} %copy-done.18, bf16[4,48,1664]{2,1,0:T(8,128)(2,1)} %copy-done.19, bf16[4,48,1664]{2,1,0:T(8,128)(2,1)} %collective-permute-done.26.refs_3_, bf16[4,48,1664]{2,1,0:T(8,128)(2,1)} %copy-done.20, ...), custom_call_target="tpu_custom_call" | custom-call | flops 4429185024 | bytes 12379136 | tf_op jit(solution)/shard_map/attn_backward/pallas_call | solution.py:355
  333.5 2.1 collective-permute-done.32
  336.9 2.1 collective-permute-done.33
  339.1 2.2 collective-permute-start.34
  341.3 1.9 collective-permute-done.34
  343.2 4.0 %collective-permute-start.35 = (bf16[50,768]{1,0:T(8,128)(2,1)S(1)}, bf16[50,768]{1,0:T(8,128)(2,1)S(1)}, u32[]{:S(2)}, u32[]{:S(2)}) collective-permute-start(bf16[50,768]{1,0:T(8,128)(2,1)S(1)} %fusion.3), channel_id=1, source_target_pairs={{0,16},{16,0},{8,24},{24,8},{1,17},{17,1},{9,25},{25,9},{2,18},{18... | collective-permute-start | bytes 230408 | tf_op jit(solution)/shard_map/ppermute | solution.py:525
  347.2 2.5 collective-permute-done.35
  349.8 5.9 %collective-permute-start.36 = (bf16[50,768]{1,0:T(8,128)(2,1)S(1)}, bf16[50,768]{1,0:T(8,128)(2,1)S(1)}, u32[]{:S(2)}, u32[]{:S(2)}) collective-permute-start(bf16[50,768]{1,0:T(8,128)(2,1)S(1)} %get-tuple-element.43), channel_id=1, source_target_pairs={{0,2},{2,0},{1,3},{3,1},{4,6},{6,4},{5,7},{7,5},{8,10},{10,8},{9,1... | collective-permute-start | bytes 230408 | tf_op jit(solution)/shard_map/ppermute | solution.py:481
  362.1 1.9 multiply_subtract_fusion
  (145 shorter events, 32.6 us)
Async XLA Ops:
  7.2 49.1 %all-gather.7.cloned.1.call-start = ((), (), s32[]{:S(2)}) async-start(), calls=%async_computation.1 | async-start | bytes 1474560 | tf_op jit(solution)/shard_map/all_gather | solution.py:559
  10.1 82.7 %all-gather.5.cloned.1.call-start = ((), (), s32[]{:S(2)}) async-start(), calls=%async_computation | async-start | bytes 2211840 | tf_op jit(solution)/shard_map/all_gather | solution.py:562
  15.8 19.3 %collective-permute-start.22 = (bf16[48,1664]{1,0:T(8,128)(2,1)S(1)}, bf16[48,1664]{1,0:T(8,128)(2,1)S(1)}, u32[]{:S(2)}, u32[]{:S(2)}) collective-permute-start(bf16[48,1664]{1,0:T(8,128)(2,1)S(1)} %get-tuple-element.60), channel_id=1, source_target_pairs={{0,16},{8,24},{16,0},{24,8},{1,17},{9,25},{17,1},{25,9},{2,18},{10... | collective-permute-start | bytes 479240 | tf_op jit(solution)/shard_map/ppermute | solution.py:502
  15.8 19.3 %collective-permute-start.21 = (bf16[48,1664]{1,0:T(8,128)(2,1)S(1)}, bf16[48,1664]{1,0:T(8,128)(2,1)S(1)}, u32[]{:S(2)}, u32[]{:S(2)}) collective-permute-start(bf16[48,1664]{1,0:T(8,128)(2,1)S(1)} %get-tuple-element.60), channel_id=1, source_target_pairs={{0,8},{8,16},{16,24},{24,0},{1,9},{9,17},{17,25},{25,1},{2,10},{10... | collective-permute-start | bytes 479240 | tf_op jit(solution)/shard_map/ppermute | solution.py:502
  35.2 10.8 %collective-permute-start.24 = (bf16[4,48,1664]{2,1,0:T(8,128)(2,1)S(1)}, bf16[4,48,1664]{2,1,0:T(8,128)(2,1)S(1)}, u32[]{:S(2)}, u32[]{:S(2)}) collective-permute-start(bf16[4,48,1664]{2,1,0:T(8,128)(2,1)S(1)} %pad_maximum_fusion.refs_0_), channel_id=1, source_target_pairs={{0,4},{1,5},{2,3},{3,2},{4,0},{5,1},{6,7},{7,6},{8,12},{9,13},{10,... | collective-permute-start | bytes 1916936 | tf_op jit(solution)/shard_map/ppermute | solution.py:495
  36.5 21.6 %collective-permute-start.25 = (bf16[4,48,1664]{2,1,0:T(8,128)(2,1)S(1)}, bf16[4,48,1664]{2,1,0:T(8,128)(2,1)S(1)}, u32[]{:S(2)}, u32[]{:S(2)}) collective-permute-start(bf16[4,48,1664]{2,1,0:T(8,128)(2,1)S(1)} %pad_maximum_fusion.refs_0_), channel_id=1, source_target_pairs={{0,1},{1,0},{2,6},{3,7},{4,5},{5,4},{6,2},{7,3},{8,9},{9,8},{10,14... | collective-permute-start | bytes 1916936 | tf_op jit(solution)/shard_map/ppermute | solution.py:495
  37.7 21.6 %collective-permute-start.27 = (bf16[4,48,1664]{2,1,0:T(8,128)(2,1)S(1)}, bf16[4,48,1664]{2,1,0:T(8,128)(2,1)S(1)}, u32[]{:S(2)}, u32[]{:S(2)}) collective-permute-start(bf16[4,48,1664]{2,1,0:T(8,128)(2,1)S(1)} %pad_maximum_fusion.refs_0_), channel_id=1, source_target_pairs={{0,2},{2,0},{1,3},{3,1},{4,6},{6,4},{5,7},{7,5},{8,10},{10,8},{9,1... | collective-permute-start | bytes 1916936 | tf_op jit(solution)/shard_map/ppermute | solution.py:481
  46.0 13.8 %collective-permute-start.26 = (bf16[4,48,1664]{2,1,0:T(8,128)(2,1)S(1)}, bf16[4,48,1664]{2,1,0:T(8,128)(2,1)}, u32[]{:S(2)}, u32[]{:S(2)}) collective-permute-start(bf16[4,48,1664]{2,1,0:T(8,128)(2,1)S(1)} %collective-permute-done.24.refs_1_), channel_id=1, source_target_pairs={{0,1},{1,0},{2,6},{3,7},{4,5},{5,4},{6,2},{7,3},{8,9},{9,8},{10,14... | collective-permute-start | bytes 1916936 | tf_op jit(solution)/shard_map/ppermute | solution.py:495
  48.2 25.5 %collective-permute-start.28 = (bf16[4,48,1664]{2,1,0:T(8,128)(2,1)S(1)}, bf16[4,48,1664]{2,1,0:T(8,128)(2,1)}, u32[]{:S(2)}, u32[]{:S(2)}) collective-permute-start(bf16[4,48,1664]{2,1,0:T(8,128)(2,1)S(1)} %collective-permute-done.24.refs_1_), channel_id=1, source_target_pairs={{0,2},{2,0},{1,3},{3,1},{4,6},{6,4},{5,7},{7,5},{8,10},{10,8},{9,1... | collective-permute-start | bytes 1916936 | tf_op jit(solution)/shard_map/ppermute | solution.py:481
  56.3 40.6 %collective-permute-start.14 = (bf16[4,48,3072]{2,1,0:T(8,128)(2,1)}, bf16[4,48,3072]{2,1,0:T(8,128)(2,1)}, u32[]{:S(2)}, u32[]{:S(2)}) collective-permute-start(bf16[4,48,3072]{2,1,0:T(8,128)(2,1)} %bitcast.71), channel_id=1, source_target_pairs={{0,4},{1,5},{2,3},{3,2},{4,0},{5,1},{6,7},{7,6},{8,12},{9,13},{10,... | collective-permute-start | bytes 3538952 | tf_op jit(solution)/shard_map/ppermute | solution.py:495
  58.0 40.1 %collective-permute-start.15 = (bf16[4,48,3072]{2,1,0:T(8,128)(2,1)}, bf16[4,48,3072]{2,1,0:T(8,128)(2,1)}, u32[]{:S(2)}, u32[]{:S(2)}) collective-permute-start(bf16[4,48,3072]{2,1,0:T(8,128)(2,1)} %bitcast.72), channel_id=1, source_target_pairs={{0,1},{1,0},{2,6},{3,7},{4,5},{5,4},{6,2},{7,3},{8,9},{9,8},{10,14... | collective-permute-start | bytes 3538952 | tf_op jit(solution)/shard_map/ppermute | solution.py:495
  59.3 39.1 %collective-permute-start.17 = (bf16[4,48,3072]{2,1,0:T(8,128)(2,1)}, bf16[4,48,3072]{2,1,0:T(8,128)(2,1)}, u32[]{:S(2)}, u32[]{:S(2)}) collective-permute-start(bf16[4,48,3072]{2,1,0:T(8,128)(2,1)} %bitcast.73), channel_id=1, source_target_pairs={{0,2},{2,0},{1,3},{3,1},{4,6},{6,4},{5,7},{7,5},{8,10},{10,8},{9,1... | collective-permute-start | bytes 3538952 | tf_op jit(solution)/shard_map/ppermute | solution.py:481
  59.8 34.1 %collective-permute-start.29 = (bf16[4,48,1664]{2,1,0:T(8,128)(2,1)S(1)}, bf16[4,48,1664]{2,1,0:T(8,128)(2,1)}, u32[]{:S(2)}, u32[]{:S(2)}) collective-permute-start(bf16[4,48,1664]{2,1,0:T(8,128)(2,1)S(1)} %collective-permute-done.25.refs_2_), channel_id=1, source_target_pairs={{0,2},{2,0},{1,3},{3,1},{4,6},{6,4},{5,7},{7,5},{8,10},{10,8},{9,1... | collective-permute-start | bytes 1916936 | tf_op jit(solution)/shard_map/ppermute | solution.py:481
  73.6 23.0 %collective-permute-start.30 = (bf16[4,48,1664]{2,1,0:T(8,128)(2,1)}, bf16[4,48,1664]{2,1,0:T(8,128)(2,1)}, u32[]{:S(2)}, u32[]{:S(2)}) collective-permute-start(bf16[4,48,1664]{2,1,0:T(8,128)(2,1)} %collective-permute-done.26.refs_3_), channel_id=1, source_target_pairs={{0,2},{2,0},{1,3},{3,1},{4,6},{6,4},{5,7},{7,5},{8,10},{10,8},{9,1... | collective-permute-start | bytes 1916936 | tf_op jit(solution)/shard_map/ppermute | solution.py:481
  93.9 10.7 %collective-permute-start.7 = (bf16[4,48,1536]{2,1,0:T(8,128)(2,1)S(1)}, bf16[4,48,1536]{2,1,0:T(8,128)(2,1)S(1)}, u32[]{:S(2)}, u32[]{:S(2)}) collective-permute-start(bf16[4,48,1536]{2,1,0:T(8,128)(2,1)S(1)} %slice.71.refs_0_), channel_id=1, source_target_pairs={{0,4},{1,5},{2,3},{3,2},{4,0},{5,1},{6,7},{7,6},{8,12},{9,13},{10,... | collective-permute-start | bytes 1769480 | tf_op jit(solution)/shard_map/ppermute | solution.py:495
  96.6 40.5 %collective-permute-start = (bf16[4,48,3072]{2,1,0:T(8,128)(2,1)S(1)}, bf16[4,48,3072]{2,1,0:T(8,128)(2,1)}, u32[]{:S(2)}, u32[]{:S(2)}) collective-permute-start(bf16[4,48,3072]{2,1,0:T(8,128)(2,1)S(1)} %slice.70.refs_0_), channel_id=1, source_target_pairs={{0,4},{1,5},{2,3},{3,2},{4,0},{5,1},{6,7},{7,6},{8,12},{9,13},{10,... | collective-permute-start | bytes 3538952 | tf_op jit(solution)/shard_map/ppermute | solution.py:495
  96.9 40.7 %collective-permute-start.1 = (bf16[4,48,3072]{2,1,0:T(8,128)(2,1)S(1)}, bf16[4,48,3072]{2,1,0:T(8,128)(2,1)S(1)}, u32[]{:S(2)}, u32[]{:S(2)}) collective-permute-start(bf16[4,48,3072]{2,1,0:T(8,128)(2,1)S(1)} %slice.70.refs_0_), channel_id=1, source_target_pairs={{0,1},{1,0},{2,6},{3,7},{4,5},{5,4},{6,2},{7,3},{8,9},{9,8},{10,14... | collective-permute-start | bytes 3538952 | tf_op jit(solution)/shard_map/ppermute | solution.py:495
  98.1 37.8 %collective-permute-start.8 = (bf16[4,48,1536]{2,1,0:T(8,128)(2,1)S(1)}, bf16[4,48,1536]{2,1,0:T(8,128)(2,1)}, u32[]{:S(2)}, u32[]{:S(2)}) collective-permute-start(bf16[4,48,1536]{2,1,0:T(8,128)(2,1)S(1)} %slice.71.refs_0_), channel_id=1, source_target_pairs={{0,1},{1,0},{2,6},{3,7},{4,5},{5,4},{6,2},{7,3},{8,9},{9,8},{10,14... | collective-permute-start | bytes 1769480 | tf_op jit(solution)/shard_map/ppermute | solution.py:495
  98.4 57.3 %collective-permute-start.16 = (bf16[4,48,3072]{2,1,0:T(8,128)(2,1)}, bf16[4,48,3072]{2,1,0:T(8,128)(2,1)}, u32[]{:S(2)}, u32[]{:S(2)}) collective-permute-start(bf16[4,48,3072]{2,1,0:T(8,128)(2,1)} %collective-permute-done.14.refs_1_), channel_id=1, source_target_pairs={{0,1},{1,0},{2,6},{3,7},{4,5},{5,4},{6,2},{7,3},{8,9},{9,8},{10,14... | collective-permute-start | bytes 3538952 | tf_op jit(solution)/shard_map/ppermute | solution.py:495
  104.7 32.4 %collective-permute-start.10 = (bf16[4,48,1536]{2,1,0:T(8,128)(2,1)S(1)}, bf16[4,48,1536]{2,1,0:T(8,128)(2,1)S(1)}, u32[]{:S(2)}, u32[]{:S(2)}) collective-permute-start(bf16[4,48,1536]{2,1,0:T(8,128)(2,1)S(1)} %slice.71.refs_0_), channel_id=1, source_target_pairs={{0,2},{2,0},{1,3},{3,1},{4,6},{6,4},{5,7},{7,5},{8,10},{10,8},{9,1... | collective-permute-start | bytes 1769480 | tf_op jit(solution)/shard_map/ppermute | solution.py:481
  135.9 18.7 %collective-permute-start.9 = (bf16[4,48,1536]{2,1,0:T(8,128)(2,1)S(1)}, bf16[4,48,1536]{2,1,0:T(8,128)(2,1)}, u32[]{:S(2)}, u32[]{:S(2)}) collective-permute-start(bf16[4,48,1536]{2,1,0:T(8,128)(2,1)S(1)} %collective-permute-done.7.refs_1_), channel_id=1, source_target_pairs={{0,1},{1,0},{2,6},{3,7},{4,5},{5,4},{6,2},{7,3},{8,9},{9,8},{10,14... | collective-permute-start | bytes 1769480 | tf_op jit(solution)/shard_map/ppermute | solution.py:495
  137.1 18.7 %collective-permute-start.11 = (bf16[4,48,1536]{2,1,0:T(8,128)(2,1)S(1)}, bf16[4,48,1536]{2,1,0:T(8,128)(2,1)S(1)}, u32[]{:S(2)}, u32[]{:S(2)}) collective-permute-start(bf16[4,48,1536]{2,1,0:T(8,128)(2,1)S(1)} %collective-permute-done.7.refs_1_), channel_id=1, source_target_pairs={{0,2},{2,0},{1,3},{3,1},{4,6},{6,4},{5,7},{7,5},{8,10},{10,8},{9,1... | collective-permute-start | bytes 1769480 | tf_op jit(solution)/shard_map/ppermute | solution.py:481
  137.1 22.8 %collective-permute-start.18 = (bf16[4,48,3072]{2,1,0:T(8,128)(2,1)}, bf16[4,48,3072]{2,1,0:T(8,128)(2,1)}, u32[]{:S(2)}, u32[]{:S(2)}) collective-permute-start(bf16[4,48,3072]{2,1,0:T(8,128)(2,1)} %collective-permute-done.14.refs_1_), channel_id=1, source_target_pairs={{0,2},{2,0},{1,3},{3,1},{4,6},{6,4},{5,7},{7,5},{8,10},{10,8},{9,1... | collective-permute-start | bytes 3538952 | tf_op jit(solution)/shard_map/ppermute | solution.py:481
  137.6 22.7 %collective-permute-start.19 = (bf16[4,48,3072]{2,1,0:T(8,128)(2,1)}, bf16[4,48,3072]{2,1,0:T(8,128)(2,1)}, u32[]{:S(2)}, u32[]{:S(2)}) collective-permute-start(bf16[4,48,3072]{2,1,0:T(8,128)(2,1)} %collective-permute-done.15.refs_2_), channel_id=1, source_target_pairs={{0,2},{2,0},{1,3},{3,1},{4,6},{6,4},{5,7},{7,5},{8,10},{10,8},{9,1... | collective-permute-start | bytes 3538952 | tf_op jit(solution)/shard_map/ppermute | solution.py:481
  154.5 15.7 %collective-permute-start.2 = (bf16[4,48,3072]{2,1,0:T(8,128)(2,1)}, bf16[4,48,3072]{2,1,0:T(8,128)(2,1)}, u32[]{:S(2)}, u32[]{:S(2)}) collective-permute-start(bf16[4,48,3072]{2,1,0:T(8,128)(2,1)} %collective-permute-done.refs_1_), channel_id=1, source_target_pairs={{0,1},{1,0},{2,6},{3,7},{4,5},{5,4},{6,2},{7,3},{8,9},{9,8},{10,14... | collective-permute-start | bytes 3538952 | tf_op jit(solution)/shard_map/ppermute | solution.py:495
  155.7 15.5 %collective-permute-start.20 = (bf16[4,48,3072]{2,1,0:T(8,128)(2,1)}, bf16[4,48,3072]{2,1,0:T(8,128)(2,1)}, u32[]{:S(2)}, u32[]{:S(2)}) collective-permute-start(bf16[4,48,3072]{2,1,0:T(8,128)(2,1)} %collective-permute-done.16.refs_3_), channel_id=1, source_target_pairs={{0,2},{2,0},{1,3},{3,1},{4,6},{6,4},{5,7},{7,5},{8,10},{10,8},{9,1... | collective-permute-start | bytes 3538952 | tf_op jit(solution)/shard_map/ppermute | solution.py:481
  159.8 75.5 %collective-permute-start.3 = (bf16[4,48,3072]{2,1,0:T(8,128)(2,1)S(1)}, bf16[4,48,3072]{2,1,0:T(8,128)(2,1)S(1)}, u32[]{:S(2)}, u32[]{:S(2)}) collective-permute-start(bf16[4,48,3072]{2,1,0:T(8,128)(2,1)S(1)} %slice.70.refs_0_), channel_id=1, source_target_pairs={{0,2},{2,0},{1,3},{3,1},{4,6},{6,4},{5,7},{7,5},{8,10},{10,8},{9,1... | collective-permute-start | bytes 3538952 | tf_op jit(solution)/shard_map/ppermute | solution.py:481
  159.9 75.4 %collective-permute-start.4 = (bf16[4,48,3072]{2,1,0:T(8,128)(2,1)}, bf16[4,48,3072]{2,1,0:T(8,128)(2,1)S(1)}, u32[]{:S(2)}, u32[]{:S(2)}) collective-permute-start(bf16[4,48,3072]{2,1,0:T(8,128)(2,1)} %collective-permute-done.refs_1_), channel_id=1, source_target_pairs={{0,2},{2,0},{1,3},{3,1},{4,6},{6,4},{5,7},{7,5},{8,10},{10,8},{9,1... | collective-permute-start | bytes 3538952 | tf_op jit(solution)/shard_map/ppermute | solution.py:481
  160.3 75.0 %collective-permute-start.5 = (bf16[4,48,3072]{2,1,0:T(8,128)(2,1)S(1)}, bf16[4,48,3072]{2,1,0:T(8,128)(2,1)S(1)}, u32[]{:S(2)}, u32[]{:S(2)}) collective-permute-start(bf16[4,48,3072]{2,1,0:T(8,128)(2,1)S(1)} %collective-permute-done.1.refs_2_), channel_id=1, source_target_pairs={{0,2},{2,0},{1,3},{3,1},{4,6},{6,4},{5,7},{7,5},{8,10},{10,8},{9,1... | collective-permute-start | bytes 3538952 | tf_op jit(solution)/shard_map/ppermute | solution.py:481
  170.2 65.1 %collective-permute-start.6 = (bf16[4,48,3072]{2,1,0:T(8,128)(2,1)}, bf16[4,48,3072]{2,1,0:T(8,128)(2,1)S(1)}, u32[]{:S(2)}, u32[]{:S(2)}) collective-permute-start(bf16[4,48,3072]{2,1,0:T(8,128)(2,1)} %collective-permute-done.2.refs_3_), channel_id=1, source_target_pairs={{0,2},{2,0},{1,3},{3,1},{4,6},{6,4},{5,7},{7,5},{8,10},{10,8},{9,1... | collective-permute-start | bytes 3538952 | tf_op jit(solution)/shard_map/ppermute | solution.py:481
  171.2 41.6 %collective-permute-start.13 = (bf16[4,48,1536]{2,1,0:T(8,128)(2,1)}, bf16[4,48,1536]{2,1,0:T(8,128)(2,1)S(1)}, u32[]{:S(2)}, u32[]{:S(2)}) collective-permute-start(bf16[4,48,1536]{2,1,0:T(8,128)(2,1)} %collective-permute-done.9.refs_3_), channel_id=1, source_target_pairs={{0,2},{2,0},{1,3},{3,1},{4,6},{6,4},{5,7},{7,5},{8,10},{10,8},{9,1... | collective-permute-start | bytes 1769480 | tf_op jit(solution)/shard_map/ppermute | solution.py:481
  349.8 10.7 %collective-permute-start.36 = (bf16[50,768]{1,0:T(8,128)(2,1)S(1)}, bf16[50,768]{1,0:T(8,128)(2,1)S(1)}, u32[]{:S(2)}, u32[]{:S(2)}) collective-permute-start(bf16[50,768]{1,0:T(8,128)(2,1)S(1)} %get-tuple-element.43), channel_id=1, source_target_pairs={{0,2},{2,0},{1,3},{3,1},{4,6},{6,4},{5,7},{7,5},{8,10},{10,8},{9,1... | collective-permute-start | bytes 230408 | tf_op jit(solution)/shard_map/ppermute | solution.py:481
  (32 other events, 761.1 us)
Sparse Core Ops, SparseCore 0:
  10.2 38.9 all-gather.6
  51.3 41.4 all-gather.4
